TPU v7x, 32 devices: a whole 2x2x4 slice. The times are simulated.
32 devices in a mesh: row: 8 (over z, core), col: 4 (over y, x).
Axes of the slice: x: 2, y: 2, z: 4, core: 2. Of those that a mesh axis runs over, the one named last changes fastest.
Arguments:
- covariance: float32 [8192, 8192], P('row', 'col'), as said below
- state_mean: float32 [8192], P('row'), may hold values from -6 to 6
- obs_values: float32 [2, 256], replicated, may hold values from -8 to 8
- obs_cells: int32 [2, 4, 256], replicated, may hold values from 0 to 8191
- obs_weights: float32 [2, 4, 256], replicated, may hold values from 0.2 to 1
- obs_variance: float32 [2, 256], replicated, may hold values from 0.05 to 1
Outputs:
- covariance_after: float32 [8192, 8192], P('row', 'col')
- state_after: float32 [8192], P('row')
Inputs may be any that keep to these rules, and one draw needn't show every extreme that they name: `covariance`: symmetric and positive definite.
All inputs are finite; a program needn't handle non-finite values.
Results may differ from a plain program's by a relative error of at most 0.0001.
Values sent between devices are 32-bit elements; how exact they have to be, the bound alone decides.
A program may use at most 64 MiB of HBM per device.

v0:
```python
import functools

import jax
import jax.numpy as jnp
from jax import lax
from jax.experimental import pallas as pl
from jax.experimental.pallas import tpu as pltpu
from jax.sharding import PartitionSpec as P

HI = lax.Precision.HIGHEST
MID = lax.Precision.HIGH
MESH = pl.DeviceIdType.MESH
BLK = 128
SUB = 8

def base_inverse(work, cols, midway):
    def panel_step(first, g, carry):
        start = pl.multiple_of(g * SUB, SUB)
        panel = work[pl.ds(start, SUB), :]
        square = pltpu.roll(panel[:, :BLK], BLK - start, 1)[:, :SUB]
        wide = [jnp.broadcast_to(square[:, j : j + 1], (SUB, BLK)) for j in range(SUB)]
        left, right = panel[:, :BLK], panel[:, BLK:]
        below = lax.broadcasted_iota(jnp.int32, (SUB, BLK), 0)
        scale = jnp.zeros((SUB, BLK), jnp.float32)
        for j in range(SUB):
            pivot = jnp.broadcast_to(wide[j][j : j + 1, :], (SUB, BLK))
            inv = 1.0 / pivot
            scale = jnp.where(below == j, lax.rsqrt(pivot), scale)
            ratio = jnp.where(below > j, wide[j] * inv, 0.0)
            left = left - ratio * left[j : j + 1, :]
            right = right - ratio * right[j : j + 1, :]
            for k in range(j + 1, SUB):
                wide[k] = wide[k] - ratio * wide[k][j : j + 1, :]
        left = left * scale
        right = right * scale
        both = jnp.concatenate([left, right], axis=1)
        lane = lax.broadcasted_iota(jnp.int32, (SUB, BLK), 1)
        lhs = jnp.where(lane >= start + SUB, left, 0.0)
        work[pl.ds(start, SUB), :] = both
        work[first:, :] = work[first:, :] - lax.dot_general(lhs[:, first:], both, (((0,), (0,)), ((), ())), precision=HI, preferred_element_type=jnp.float32)
        return carry
    steps = BLK // SUB // 4
    for quarter in range(4):
        if quarter == 2:
            midway()
        first = quarter * steps * SUB
        lax.fori_loop(quarter * steps, (quarter + 1) * steps, functools.partial(panel_step, first), 0)

def factor_inverse(mat, work, cols, between):
    size = mat.shape[0]
    eye = (lax.broadcasted_iota(jnp.int32, (BLK, BLK), 0) == lax.broadcasted_iota(jnp.int32, (BLK, BLK), 1)).astype(jnp.float32)
    for b in range(size // BLK):
        lo, hi = b * BLK, (b + 1) * BLK
        work[:, :BLK] = mat[lo:hi, lo:hi]
        work[:, BLK:] = eye
        base_inverse(work, cols, lambda: between(2 * b + 1))
        winv = work[:, BLK:]
        if hi < size:
            panel = jnp.dot(winv, mat[lo:hi, hi:size], precision=HI, preferred_element_type=jnp.float32)
        if lo > 0:
            left = jnp.dot(winv, mat[lo:hi, size : size + lo], precision=HI, preferred_element_type=jnp.float32)
            mat[lo:hi, size : size + lo] = left
        mat[lo:hi, size + lo : size + hi] = winv
        if hi < size:
            right = mat[lo:hi, size : size + hi]
            dims = (((0,), (0,)), ((), ()))
            mat[hi:size, hi:size] = mat[hi:size, hi:size] - lax.dot_general(panel, panel, dims, precision=HI, preferred_element_type=jnp.float32)
            mat[hi:size, size : size + hi] = mat[hi:size, size : size + hi] - lax.dot_general(panel, right, dims, precision=HI, preferred_element_type=jnp.float32)
        between(2 * b + 2)


def pair_blocks(size):
    count = size // BLK
    return [(i, j) for i in range(count) for j in range(i + 1)]


def kernel(
    nr, nc, t_ref, op_ref, part_ref, var_ref, inv_ref, gain_ref, xc_ref, pred_ref,
    xr_ref, acc, full, land, tland, mat, work, cols, send_sem, recv_sem,
):
    ratio = nr // nc
    row, col = lax.axis_index("row"), lax.axis_index("col")
    high, low = row // ratio, row % ratio
    packed = acc.shape[0]
    rows, size = t_ref.shape
    chunk = rows // nc
    sub = chunk // 2
    pieces = 2 * nc
    used = [0]

    def take(count):
        used[0] += count
        return used[0] - count

    levels = [
        (ratio, low, lambda d: (high * ratio + lax.rem(low + d, ratio), col)),
        (nc, col, lambda d: (row, lax.rem(col + d, nc))),
        (nc, high, lambda d: (lax.rem(high + d, nc) * ratio + low, col)),
    ]
    barrier = pltpu.get_barrier_semaphore()
    for n, me, peer in levels:
        for d in range(1, n):
            pl.semaphore_signal(barrier, inc=1, device_id=peer(d), device_id_type=MESH)
    pl.semaphore_wait(barrier, ratio - 1 + 2 * (nc - 1))

    def remote(src, dst, sem, device):
        return pltpu.make_async_remote_copy(
            src_ref=src, dst_ref=dst, send_sem=send_sem.at[sem], recv_sem=recv_sem.at[sem],
            device_id=device, device_id_type=MESH,
        )

    t_base = take(2 * (nc - 1))
    _, _, col_peer = levels[1]
    t_copies = []
    for h in range(2):
        for d in range(1, nc):
            other = lax.rem(col + d, nc)
            src = t_ref.at[pl.ds(pl.multiple_of(other * chunk + h * sub, 8), sub)]
            dst = tland.at[d - 1, pl.ds(h * sub, sub)]
            t_copies.append(remote(src, dst, t_base + h * (nc - 1) + d - 1, col_peer(d)))
    for copy in t_copies[: nc - 1]:
        copy.start()

    gather_base = take(2 * (nc - 1))
    chain_base = take(pieces)
    down_base = take(pieces)
    sib_base = take(pieces * (ratio - 1))
    gathers = []
    for h in range(2):
        for d in range(1, nc):
            own = xr_ref.at[pl.ds(pl.multiple_of(col * chunk + h * sub, 8), sub)]
            gathers.append(remote(own, own, gather_base + h * (nc - 1) + d - 1, col_peer(d)))
    _, _, low_peer = levels[0]
    source = high == col
    top = nc - 1
    above = (jnp.minimum(high + 1, top) * ratio + low, col)
    below = (jnp.maximum(high - 1, 0) * ratio + low, col)
    goes_up = jnp.logical_and(high >= col, high < top)
    goes_down = jnp.logical_and(high <= col, high > 0)
    onward = jnp.logical_or(goes_up, goes_down)
    middle = jnp.logical_and(onward, jnp.logical_not(source))
    last = jnp.logical_and(jnp.logical_not(onward), jnp.logical_not(source))

    spot = [(0, 0), (0, 1)] + [(d, h) for h in range(2) for d in range(1, nc)]

    def links(e, src_is_own):
        begin = pl.multiple_of(lax.rem(col - spot[e][0] + nc, nc) * chunk + spot[e][1] * sub, 8)
        dst = xc_ref.at[low, pl.ds(begin, sub)]
        src = xr_ref.at[pl.ds(begin, sub)] if src_is_own else dst
        up = remote(src, dst, chain_base + e, above)
        down = pltpu.make_async_remote_copy(
            src_ref=src, dst_ref=dst, send_sem=send_sem.at[down_base + e],
            recv_sem=recv_sem.at[chain_base + e], device_id=below, device_id_type=MESH,
        )
        sibs = [remote(src, dst, sib_base + e * (ratio - 1) + q - 1, low_peer(q)) for q in range(1, ratio)]
        return begin, up, down, sibs

    def send_on(up, down, sibs):
        @pl.when(goes_up)
        def _():
            up.start()

        @pl.when(goes_down)
        def _():
            down.start()

        for sib in sibs:
            sib.start()

    def relay_source(e):
        if e >= 2:
            gathers[e - 2].wait_recv()
        begin, up, down, sibs = links(e, True)
        send_on(up, down, sibs if e >= 2 else [])
        xc_ref[low, pl.ds(begin, sub), :] = xr_ref[pl.ds(begin, sub), :]

    def relay_middle(e):
        begin, up, down, sibs = links(e, False)
        up.wait_recv()
        send_on(up, down, sibs)

    def relay_last(e):
        begin, up, down, sibs = links(e, False)
        up.wait_recv()
        for sib in sibs:
            sib.start()

    near = jnp.abs(high - col) == 1

    def between(slot):
        @pl.when(source)
        def _():
            if slot == 0:
                for e in range(2):
                    for sib in links(e, True)[3]:
                        sib.start()
                relay_source(2)
            if slot + 3 < pieces:
                relay_source(slot + 3)

        @pl.when(jnp.logical_and(middle, near))
        def _():
            if slot == 0:
                relay_middle(0)
            if slot + 1 < pieces:
                relay_middle(slot + 1)

        @pl.when(jnp.logical_and(middle, jnp.logical_not(near)))
        def _():
            if 0 <= slot - 1 < pieces - 1:
                relay_middle(slot - 1)
            if slot == pieces - 1:
                relay_middle(pieces - 1)

        @pl.when(last)
        def _():
            if 0 <= slot - 2 < pieces:
                relay_last(slot - 2)

    def owned(h):
        for copy in t_copies[h * (nc - 1) : (h + 1) * (nc - 1)]:
            copy.wait()
        where = pl.ds(pl.multiple_of(col * chunk + h * sub, 8), sub)
        total = t_ref[where, :]
        for d in range(1, nc):
            total = total + tland[d - 1, h * sub : (h + 1) * sub, :]
        xr_ref[where, :] = total

        @pl.when(source)
        def _():
            relay_source(h)

    place = 0
    for i in range(size // BLK):
        block = lax.dot_general(
            op_ref[:, i * BLK : (i + 1) * BLK], t_ref[:, : (i + 1) * BLK], (((0,), (0,)), ((), ())),
            precision=MID, preferred_element_type=jnp.float32,
        )
        for j in range(i + 1):
            acc[place : place + BLK, :] = block[:, j * BLK : (j + 1) * BLK]
            place += BLK
    acc[place : place + 8, :] = part_ref[...]
    acc[place + 8 :, :] = jnp.zeros((packed - place - 8, BLK), jnp.float32)
    start, length, slot = 0, packed, 0
    spots = []
    for level, (n, me, peer) in enumerate(levels):
        part = length // n
        base = take(n - 1)
        copies = []
        for d in range(1, n):
            other = lax.rem(me + d, n)
            src = acc.at[pl.ds(pl.multiple_of(start + other * part, 8), part)]
            dst = land.at[pl.ds(slot + (d - 1) * part, part)]
            copies.append(remote(src, dst, base + d - 1, peer(d)))
            copies[-1].start()
        if level == 1:
            for copy in t_copies[nc - 1 :]:
                copy.start()
        start = pl.multiple_of(start + me * part, 8)
        length = part
        spots.append((start, part))
        for copy in copies:
            copy.wait()
        mine = acc[pl.ds(start, part), :]
        for d in range(1, n):
            mine = mine + land[pl.ds(slot + (d - 1) * part, part), :]
        acc[pl.ds(start, part), :] = mine
        slot += (n - 1) * part
    full[pl.ds(start, length), :] = acc[pl.ds(start, length), :]

    for level in (2, 1, 0):
        n, me, peer = levels[level]
        begin, part = spots[level]
        base = take(n - 1)
        copies = []
        for d in range(1, n):
            where = full.at[pl.ds(begin, part)]
            copies.append(remote(where, where, base + d - 1, peer(d)))
            copies[-1].start()
        if level == 1:
            owned(1)
            for copy in gathers:
                copy.start()
        for copy in copies:
            copy.wait()
        if level == 2:
            owned(0)

    same = lax.broadcasted_iota(jnp.int32, (BLK, BLK), 0) == lax.broadcasted_iota(jnp.int32, (BLK, BLK), 1)
    for index, (i, j) in enumerate(pair_blocks(size)):
        block = full[index * BLK : (index + 1) * BLK, :]
        if i == j:
            block = 0.5 * (block + block.T) + jnp.where(same, var_ref[:, i * BLK : (i + 1) * BLK], 0.0)
        mat[i * BLK : (i + 1) * BLK, j * BLK : (j + 1) * BLK] = block
        if i != j:
            mat[j * BLK : (j + 1) * BLK, i * BLK : (i + 1) * BLK] = block.T
    mat[:, size:] = jnp.zeros((size, size), jnp.float32)
    tail = len(pair_blocks(size)) * BLK
    pred_ref[...] = full[tail : tail + 8, :]

    between(0)
    factor_inverse(mat, work, cols, between)
    inverse = mat[:, size:]
    inv_ref[...] = inverse
    for copy in gathers:
        copy.wait_send()

    @pl.when(jnp.logical_not(source))
    def _():
        for copy in gathers:
            copy.wait_recv()

    for slot in range(2 * (size // BLK) + 1, pieces):
        between(slot)
    gain_ref[...] = lax.dot_general(
        xr_ref[...], inverse, (((1,), (1,)), ((), ())), precision=MID, preferred_element_type=jnp.float32
    )
    for slot in range(max(pieces, 2 * (size // BLK) + 1), pieces + 2):
        between(slot)

    for e in range(pieces):
        _, up, down, sibs = links(e, False)

        @pl.when(goes_up)
        def _():
            up.wait_send()

        @pl.when(goes_down)
        def _():
            down.wait_send()

        for sib in sibs:
            sib.wait()


def exchange(mesh, total, part, row_op, part_pred, variance):
    nr, nc = mesh.shape["row"], mesh.shape["col"]
    ratio = nr // nc
    rows, size = part.shape
    landing, length = 0, total
    for n in (ratio, nc, nc):
        landing += (n - 1) * (length // n)
        length //= n
    sems = 2 * (ratio - 1 + 2 * (nc - 1)) + 4 * (nc - 1) + 4 * nc + 2 * nc * (ratio - 1)
    f32 = jnp.float32
    vmem = pl.BlockSpec(memory_space=pltpu.VMEM)
    return pl.pallas_call(
        functools.partial(kernel, nr, nc),
        out_shape=(
            jax.ShapeDtypeStruct((size, size), f32),
            jax.ShapeDtypeStruct((rows, size), f32),
            jax.ShapeDtypeStruct((ratio, rows, size), f32),
            jax.ShapeDtypeStruct((8, BLK), f32),
        ),
        in_specs=[vmem] * 4,
        out_specs=(vmem,) * 4,
        scratch_shapes=[
            pltpu.VMEM((rows, size), f32),
            pltpu.VMEM((total, BLK), f32),
            pltpu.VMEM((total, BLK), f32),
            pltpu.VMEM((landing, BLK), f32),
            pltpu.VMEM((nc - 1, rows // nc, size), f32),
            pltpu.VMEM((size, 2 * size), f32),
            pltpu.VMEM((BLK, 2 * BLK), f32),
            pltpu.VMEM((BLK, BLK), f32),
            pltpu.SemaphoreType.DMA((sems,)),
            pltpu.SemaphoreType.DMA((sems,)),
        ],
        compiler_params=pltpu.CompilerParams(collective_id=0, has_side_effects=True, vmem_limit_bytes=40 * 1024 * 1024),
    )(part, row_op, part_pred, variance)


def dot(a, b, precision):
    return jnp.dot(a, b, precision=precision, preferred_element_type=jnp.float32)


def local_operator(cells, weights, start, count):
    positions = start + lax.iota(jnp.int32, count)[:, None]
    total = jnp.zeros((count, cells.shape[1]), jnp.float32)
    for foot in range(cells.shape[0]):
        total = total + jnp.where(cells[foot][None, :] == positions, weights[foot][None, :], 0.0)
    return total


def on_device(mesh, covariance, state_mean, obs_values, obs_cells, obs_weights, obs_variance):
    rows_dev, cols_dev = covariance.shape
    row_index = lax.axis_index("row")
    col_index = lax.axis_index("col")
    devices = mesh.shape["row"] * mesh.shape["col"]
    batches, foot, width = obs_cells.shape
    total = batches * width
    cells = obs_cells.transpose(1, 0, 2).reshape(foot, total)
    weights = obs_weights.transpose(1, 0, 2).reshape(foot, total)
    values = obs_values.reshape(total)
    variance = obs_variance.reshape(1, total)
    col_op = local_operator(cells, weights, col_index * cols_dev, cols_dev)
    row_op = local_operator(cells, weights, row_index * rows_dev, rows_dev)
    part = dot(covariance, col_op, MID)
    part_pred = jnp.sum(row_op * state_mean[:, None], axis=0)
    part_pred = jnp.where(col_index == 0, part_pred, 0.0).reshape(total // BLK, BLK)
    part_pred = jnp.pad(part_pred, ((0, 8 - total // BLK), (0, 0)))
    filled = len(pair_blocks(total)) * BLK + 8
    unit = 8 * devices
    packed = -(-(filled + 8) // unit) * unit
    inverse, gain, cross_cols, pred = exchange(mesh, packed, part, row_op, part_pred, variance)
    predicted = pred[: total // BLK].reshape(total)
    innov = values - predicted
    white = jnp.sum(inverse * innov[None, :], axis=1)
    gain_cols = dot(cross_cols.reshape(cols_dev, total), inverse.T, MID)
    mean = state_mean + jnp.sum(gain * white[None, :], axis=1)
    matrix = covariance - dot(gain, gain_cols.T, MID)
    return (matrix, mean)


def solution(mesh):
    return jax.shard_map(
        functools.partial(on_device, mesh),
        mesh=mesh,
        in_specs=(P("row", "col"), P("row"), P(), P(), P(), P()),
        out_specs=(P("row", "col"), P("row")),
        check_vma=False,
    )
```

profile of v0, /device:TPU:7, one launch (start us, length us, event | category | flops | bytes accessed | tf_op | source)
XLA Modules:
  0.0 129.8 jit_solution(9097348607479517674)
XLA Ops:
  0.6 0.7 copy.11
  1.3 0.7 copy.10
  2.0 0.9 fusion.26
  2.9 0.9 fusion.27
  3.7 0.0 copy-start
  3.7 10.7 %fusion.22.t_ref = f32[1024,512]{1,0:T(8,128)S(1)} fusion(f32[1024,2048]{1,0:T(8,128)} %param.6, f32[512]{0:T(512)S(1)} %bitcast.41, s32[512]{0:T(512)S(1)} %bitcast.33, f32[512]{0:T(512)S(1)} %bitcast.43, s32[512]{0:T(512)S(1)} %bitcast.35, f32[512]{0:T(512)S(1)} %bitcast.45, s32[512]{0:T(512)S(1)} %bitcast.37, f32[512]{0:T(512)S(1)} %bitcast.39, ...), kind=kOutput, calls=%fused_computation.26 | convolution fusion | flops 6453985280 | bytes 10510336 | tf_op jit(solution)/shard_map/dot_general | solution.py:374
  14.4 0.0 copy-done
  14.4 1.0 multiply_reduce_fusion.1
  15.4 0.0 slice-start
  15.4 100.1 %shard_map.77 = (f32[512,512]{1,0:T(8,128)S(1)}, f32[1024,512]{1,0:T(8,128)S(1)}, f32[2,1024,512]{2,1,0:T(8,128)S(1)}, f32[8,128]{1,0:T(8,128)S(1)}) custom-call(f32[1024,512]{1,0:T(8,128)S(1)} %fusion.22.t_ref, f32[1024,512]{1,0:T(8,128)S(1)} %get-tuple-element.11.op_ref, f32[8,128]{1,0:T(8,128)S(1)} %pad.4.part_ref, f32[1,512]{1,0:T(1,128)S(1)} %bitcast.28), custom_call_target="tpu_custom_call" | custom-call | tf_op jit(solution)/shard_map/pallas_call | solution.py:347
  115.5 0.0 slice-start.1
  115.6 3.6 %fusion.28 = f32[2048,512]{1,0:T(8,128)S(1)} fusion(f32[2048,512]{1,0:T(8,128)S(1)} %bitcast.27, f32[512,512]{1,0:T(8,128)S(1)} %get-tuple-element.8), kind=kOutput, calls=%fused_computation.35 | convolution fusion | flops 3221225472 | bytes 9437184 | tf_op jit(solution)/shard_map/dot_general | solution.py:374
  119.2 0.2 multiply_reduce_fusion.2
  119.4 0.2 multiply_reduce_fusion
  119.6 0.6 add.55
  120.2 0.0 slice-done
  120.2 0.0 slice-done.1
  120.2 9.6 %convolution_subtract_fusion = f32[1024,2048]{1,0:T(8,128)} fusion(f32[1024,2048]{1,0:T(8,128)S(1)} %bitcast.30, f32[1024,512]{1,0:T(8,128)S(1)} %get-tuple-element.6, f32[2048,512]{1,0:T(8,128)S(1)} %fusion.28), kind=kOutput, calls=%fused_computation.12 | convolution fusion | flops 6444548096 | bytes 23068672 | tf_op jit(solution)/shard_map/dot_general | solution.py:374
  (6 shorter events, 0.0 us)
Async XLA Ops:
  3.7 10.7 %copy-start = (f32[1024]{0:T(1024)S(1)}, f32[1024]{0:T(1024)}, u32[]{:S(2)}) copy-start(f32[1024]{0:T(1024)} %param.7) | copy-start | bytes 12292
  15.4 104.8 %slice-start = ((s8[8388608]{0:T(1024)(128)(4,1)}), s8[4194304]{0:T(1024)(128)(4,1)S(1)}, s32[]{:S(2)}) async-start(s8[8388608]{0:T(1024)(128)(4,1)} %bitcast.29), calls=%async_computation | async-start | bytes 8388608
  115.5 4.7 %slice-start.1 = ((s8[8388608]{0:T(1024)(128)(4,1)}), s8[4194304]{0:T(1024)(128)(4,1)S(1)}, s32[]{:S(2)}) async-start(s8[8388608]{0:T(1024)(128)(4,1)} %bitcast.29), calls=%async_computation.1 | async-start | bytes 8388608
where the time goes:
time: 131 us; the launch traced here: 130 us
  Pallas kernels  100 us (76%)
  matrix products  23.9 us (18%)
  local copies, waits for them, and re-layouts  3.11 us (2%)
  other arithmetic  1.96 us (1%)
    pallas_call x1, Pallas kernels, exchange(): pl.pallas_call(functools.partial(kernel, nr, nc), out_shape=(jax.ShapeDty...  100 us
    dot_general x3, matrix products, dot(): jnp.dot(a, b, precision=precision, preferred_element_type=jnp.float32)  23.9 us

commit v1 on v0

v1 whole, which is shorter than its diff:
```python
import functools

import jax
import jax.numpy as jnp
from jax import lax
from jax.experimental import pallas as pl
from jax.experimental.pallas import tpu as pltpu
from jax.sharding import PartitionSpec as P

HI = lax.Precision.HIGHEST
MID = lax.Precision.HIGH
MESH = pl.DeviceIdType.MESH
BLK = 128
SUB = 8

def base_inverse(work, hook):
    def panel_step(first, g, carry):
        start = pl.multiple_of(g * SUB, SUB)
        panel = work[pl.ds(start, SUB), :]
        square = pltpu.roll(panel[:, :BLK], BLK - start, 1)[:, :SUB]
        wide = [jnp.broadcast_to(square[:, j : j + 1], (SUB, BLK)) for j in range(SUB)]
        left, right = panel[:, :BLK], panel[:, BLK:]
        below = lax.broadcasted_iota(jnp.int32, (SUB, BLK), 0)
        scale = jnp.zeros((SUB, BLK), jnp.float32)
        for j in range(SUB):
            pivot = jnp.broadcast_to(wide[j][j : j + 1, :], (SUB, BLK))
            inv = 1.0 / pivot
            scale = jnp.where(below == j, lax.rsqrt(pivot), scale)
            ratio = jnp.where(below > j, wide[j] * inv, 0.0)
            left = left - ratio * left[j : j + 1, :]
            right = right - ratio * right[j : j + 1, :]
            for k in range(j + 1, SUB):
                wide[k] = wide[k] - ratio * wide[k][j : j + 1, :]
        left = left * scale
        right = right * scale
        both = jnp.concatenate([left, right], axis=1)
        lane = lax.broadcasted_iota(jnp.int32, (SUB, BLK), 1)
        lhs = jnp.where(lane >= start + SUB, left, 0.0)
        work[pl.ds(start, SUB), :] = both
        work[first:, :] = work[first:, :] - lax.dot_general(lhs[:, first:], both, (((0,), (0,)), ((), ())), precision=HI, preferred_element_type=jnp.float32)
        return carry
    steps = BLK // SUB // 4
    for quarter in range(4):
        hook(quarter)
        first = quarter * steps * SUB
        lax.fori_loop(quarter * steps, (quarter + 1) * steps, functools.partial(panel_step, first), 0)

def factor_inverse(mat, work, hook):
    size = mat.shape[0]
    eye = (lax.broadcasted_iota(jnp.int32, (BLK, BLK), 0) == lax.broadcasted_iota(jnp.int32, (BLK, BLK), 1)).astype(jnp.float32)
    for b in range(size // BLK):
        lo, hi = b * BLK, (b + 1) * BLK
        work[:, :BLK] = mat[lo:hi, lo:hi]
        work[:, BLK:] = eye
        base_inverse(work, lambda quarter: hook(4 * b + quarter))
        winv = work[:, BLK:]
        if hi < size:
            panel = jnp.dot(winv, mat[lo:hi, hi:size], precision=HI, preferred_element_type=jnp.float32)
        if lo > 0:
            left = jnp.dot(winv, mat[lo:hi, size : size + lo], precision=HI, preferred_element_type=jnp.float32)
            mat[lo:hi, size : size + lo] = left
        mat[lo:hi, size + lo : size + hi] = winv
        if hi < size:
            right = mat[lo:hi, size : size + hi]
            dims = (((0,), (0,)), ((), ()))
            mat[hi:size, hi:size] = mat[hi:size, hi:size] - lax.dot_general(panel, panel, dims, precision=HI, preferred_element_type=jnp.float32)
            mat[hi:size, size : size + hi] = mat[hi:size, size : size + hi] - lax.dot_general(panel, right, dims, precision=HI, preferred_element_type=jnp.float32)


def pair_blocks(size):
    count = size // BLK
    return [(i, j) for i in range(count) for j in range(i + 1)]


def split(value):
    high = value.astype(jnp.bfloat16)
    return high, (value - high.astype(jnp.float32)).astype(jnp.bfloat16)


def matmul(a, b, dims=(((1,), (0,)), ((), ()))):
    return lax.dot_general(a, b, dims, preferred_element_type=jnp.float32)


def part_count(rows, nc):
    return 4 if rows % (4 * nc * SUB) == 0 else 2


def relay_order(nc, parts):
    order = []
    for pair in range(0, parts, 2):
        order += [(0, pair), (0, pair + 1)]
        order += [(d, h) for h in (pair, pair + 1) for d in range(1, nc)]
    return order


def kernel(
    nr, nc, parts, p_ref, x_ref, cells_ref, weights_ref, var_ref, u_ref, xc_ref, pred_ref,
    block, high_op, low_op, row_op, t_ref, xr_ref, acc, full, land, tland, mat, work, send_sem, recv_sem, load_sem,
):
    ratio = nr // nc
    row, col = lax.axis_index("row"), lax.axis_index("col")
    high, low = row // ratio, row % ratio
    packed = acc.shape[0]
    rows, size = t_ref.shape
    wide = block.shape[1]
    part = rows // parts
    sub = part // nc
    order = relay_order(nc, parts)
    pieces = len(order)
    used = [0]

    def take(count):
        used[0] += count
        return used[0] - count

    loads = []
    for h in range(parts):
        where = pl.ds(h * part, part)
        loads.append(pltpu.make_async_copy(p_ref.at[where], block.at[where], load_sem.at[h]))
        loads[-1].start()

    levels = [
        (ratio, low, lambda d: (high * ratio + lax.rem(low + d, ratio), col)),
        (nc, col, lambda d: (row, lax.rem(col + d, nc))),
        (nc, high, lambda d: (lax.rem(high + d, nc) * ratio + low, col)),
    ]
    barrier = pltpu.get_barrier_semaphore()
    for n, me, peer in levels:
        for d in range(1, n):
            pl.semaphore_signal(barrier, inc=1, device_id=peer(d), device_id_type=MESH)

    def operator(first, count, store):
        step = min(count, BLK)
        batches, foot, width = cells_ref.shape

        def fill(g, carry):
            start = pl.multiple_of(g * step, step)
            place = lax.broadcasted_iota(jnp.int32, (step, width), 0) + (first + start)
            for b in range(batches):
                total = jnp.zeros((step, width), jnp.float32)
                for f in range(foot):
                    total = total + jnp.where(cells_ref[b, f : f + 1, :] == place, weights_ref[b, f : f + 1, :], 0.0)
                store(start, step, b * width, width, total)
            return carry

        lax.fori_loop(0, count // step, fill, 0)

    def store_col(start, step, lane, width, total):
        h, l = split(total)
        high_op[pl.ds(start, step), lane : lane + width] = h
        low_op[pl.ds(start, step), lane : lane + width] = l

    def store_row(start, step, lane, width, total):
        row_op[pl.ds(start, step), lane : lane + width] = total

    operator(col * wide, wide, store_col)

    def remote(src, dst, sem, device):
        return pltpu.make_async_remote_copy(
            src_ref=src, dst_ref=dst, send_sem=send_sem.at[sem], recv_sem=recv_sem.at[sem],
            device_id=device, device_id_type=MESH,
        )

    def own_rows(h, owner):
        return pl.ds(pl.multiple_of(h * part + owner * sub, 8), sub)

    _, _, col_peer = levels[1]
    _, _, low_peer = levels[0]
    t_base = take(parts * (nc - 1))
    gather_base = take(parts * (nc - 1))
    chain_base = take(pieces)
    down_base = take(pieces)
    sib_base = take(pieces * (ratio - 1))
    t_copies, gathers = [], []
    for h in range(parts):
        t_copies.append([])
        gathers.append([])
        for d in range(1, nc):
            src = t_ref.at[own_rows(h, lax.rem(col + d, nc))]
            dst = tland.at[d - 1, pl.ds(h * sub, sub)]
            t_copies[h].append(remote(src, dst, t_base + h * (nc - 1) + d - 1, col_peer(d)))
            own = xr_ref.at[own_rows(h, col)]
            gathers[h].append(remote(own, own, gather_base + h * (nc - 1) + d - 1, col_peer(d)))

    def start_all(copies):
        for copy in copies:
            copy.start()

    source = high == col
    far = jnp.abs(high - col)
    top = nc - 1
    above = (jnp.minimum(high + 1, top) * ratio + low, col)
    below = (jnp.maximum(high - 1, 0) * ratio + low, col)
    goes_up = jnp.logical_and(high >= col, high < top)
    goes_down = jnp.logical_and(high <= col, high > 0)

    def links(e, src_is_own):
        d, h = order[e]
        where = own_rows(h, lax.rem(col - d + nc, nc))
        dst = xc_ref.at[low, where]
        src = xr_ref.at[where] if src_is_own else dst
        up = remote(src, dst, chain_base + e, above)
        down = pltpu.make_async_remote_copy(
            src_ref=src, dst_ref=dst, send_sem=send_sem.at[down_base + e],
            recv_sem=recv_sem.at[chain_base + e], device_id=below, device_id_type=MESH,
        )
        sibs = [remote(src, dst, sib_base + e * (ratio - 1) + q - 1, low_peer(q)) for q in range(1, ratio)]
        return where, up, down, sibs

    def send_on(up, down, sibs):
        @pl.when(goes_up)
        def _():
            up.start()

        @pl.when(goes_down)
        def _():
            down.start()

        for sib in sibs:
            sib.start()

    def relay_source(e):
        d, h = order[e]
        if d > 0:
            gathers[h][d - 1].wait_recv()
        where, up, down, sibs = links(e, True)
        send_on(up, down, sibs)
        xc_ref[low, where, :] = xr_ref[where, :]

    def relay(e):
        where, up, down, sibs = links(e, False)
        up.wait_recv()
        send_on(up, down, sibs)

    def owned(h):
        for copy in t_copies[h]:
            copy.wait()
        where = own_rows(h, col)
        total = t_ref[where, :]
        for d in range(1, nc):
            total = total + tland[d - 1, h * sub : (h + 1) * sub, :]
        xr_ref[where, :] = total

    late = order.index((0, 2)) if parts > 2 else -1

    def service(k):
        if parts > 2:
            if k == late:
                owned(2)
                start_all(gathers[2])
            if k == late + 1:
                owned(3)
                start_all(gathers[3])
        for test, lag, act in ((far == 0, 0, relay_source), (far == 1, 2, relay), (far == 2, 4, relay), (far > 2, 6, relay)):
            if 0 <= k - lag < pieces:
                pl.when(test)(functools.partial(act, k - lag))

    for h in range(parts):
        loads[h].wait()
        where = slice(h * part, (h + 1) * part)
        a, b = split(block[where, :])
        t_ref[where, :] = matmul(a, high_op[...]) + matmul(a, low_op[...]) + matmul(b, high_op[...])
        if h == 0:
            pl.semaphore_wait(barrier, ratio - 1 + 2 * (nc - 1))
        if h < 2:
            start_all(t_copies[h])
        if h == parts - 2:
            operator(row * rows, rows, store_row)

    place = 0
    for i in range(size // BLK):
        blocks = lax.dot_general(
            row_op[:, i * BLK : (i + 1) * BLK], t_ref[:, : (i + 1) * BLK], (((0,), (0,)), ((), ())),
            precision=MID, preferred_element_type=jnp.float32,
        )
        for j in range(i + 1):
            acc[place : place + BLK, :] = blocks[:, j * BLK : (j + 1) * BLK]
            place += BLK
    predicted = jnp.dot(x_ref[...], row_op[...], precision=HI, preferred_element_type=jnp.float32)
    predicted = jnp.where(col == 0, predicted, 0.0)
    acc[place:, :] = jnp.zeros((packed - place, BLK), jnp.float32)
    for i in range(size // BLK):
        acc[place + i : place + i + 1, :] = predicted[:, i * BLK : (i + 1) * BLK]
    start, length, slot = 0, packed, 0
    spots = []
    for level, (n, me, peer) in enumerate(levels):
        segment = length // n
        base = take(n - 1)
        copies = []
        for d in range(1, n):
            other = lax.rem(me + d, n)
            src = acc.at[pl.ds(pl.multiple_of(start + other * segment, 8), segment)]
            dst = land.at[pl.ds(slot + (d - 1) * segment, segment)]
            copies.append(remote(src, dst, base + d - 1, peer(d)))
            copies[-1].start()
        if level == 0:
            owned(0)
        if level == 1:
            owned(1)
            start_all(gathers[0])
        if level == 2:
            start_all(gathers[1])
        service(level)
        start = pl.multiple_of(start + me * segment, 8)
        length = segment
        spots.append((start, segment))
        for copy in copies:
            copy.wait()
        mine = acc[pl.ds(start, segment), :]
        for d in range(1, n):
            mine = mine + land[pl.ds(slot + (d - 1) * segment, segment), :]
        acc[pl.ds(start, segment), :] = mine
        slot += (n - 1) * segment
    full[pl.ds(start, length), :] = acc[pl.ds(start, length), :]

    for level in (2, 1, 0):
        n, me, peer = levels[level]
        begin, segment = spots[level]
        base = take(n - 1)
        copies = []
        for d in range(1, n):
            where = full.at[pl.ds(begin, segment)]
            copies.append(remote(where, where, base + d - 1, peer(d)))
            copies[-1].start()
        if level == 1:
            for h in range(2, parts):
                start_all(t_copies[h])
        service(5 - level)
        for copy in copies:
            copy.wait()

    same = lax.broadcasted_iota(jnp.int32, (BLK, BLK), 0) == lax.broadcasted_iota(jnp.int32, (BLK, BLK), 1)
    width = var_ref.shape[1]
    for index, (i, j) in enumerate(pair_blocks(size)):
        square = full[index * BLK : (index + 1) * BLK, :]
        if i == j:
            lane = i * BLK % width
            diagonal = var_ref[i * BLK // width : i * BLK // width + 1, lane : lane + BLK]
            square = 0.5 * (square + square.T) + jnp.where(same, diagonal, 0.0)
        mat[i * BLK : (i + 1) * BLK, j * BLK : (j + 1) * BLK] = square
        if i != j:
            mat[j * BLK : (j + 1) * BLK, i * BLK : (i + 1) * BLK] = square.T
    mat[:, size:] = jnp.zeros((size, size), jnp.float32)
    tail = len(pair_blocks(size)) * BLK
    pred_ref[...] = full[tail : tail + 8, :]

    factor_inverse(mat, work, lambda slot: service(slot + 6))
    for k in range(6 + 4 * (size // BLK), pieces + 6):
        service(k)
    for h in range(parts):
        for copy in gathers[h]:
            copy.wait_send()

    @pl.when(jnp.logical_not(source))
    def _():
        for h in range(parts):
            for copy in gathers[h]:
                copy.wait_recv()

    inverse = mat[:, size:]
    gain = lax.dot_general(
        xr_ref[...], inverse, (((1,), (1,)), ((), ())), precision=MID, preferred_element_type=jnp.float32
    )
    u_ref[...] = jnp.dot(gain, inverse, precision=MID, preferred_element_type=jnp.float32)

    for e in range(pieces):
        _, up, down, sibs = links(e, False)

        @pl.when(goes_up)
        def _():
            up.wait_send()

        @pl.when(goes_down)
        def _():
            down.wait_send()

        for sib in sibs:
            sib.wait()


def exchange(mesh, packed, covariance, state, cells, weights, variance):
    nr, nc = mesh.shape["row"], mesh.shape["col"]
    ratio = nr // nc
    rows, cols = covariance.shape
    size = cells.shape[0] * cells.shape[2]
    parts = part_count(rows, nc)
    landing, length = 0, packed
    for n in (ratio, nc, nc):
        landing += (n - 1) * (length // n)
        length //= n
    pieces = nc * parts
    sems = 2 * (ratio - 1 + 2 * (nc - 1)) + 2 * parts * (nc - 1) + 2 * pieces + pieces * (ratio - 1)
    f32 = jnp.float32
    vmem = pl.BlockSpec(memory_space=pltpu.VMEM)
    return pl.pallas_call(
        functools.partial(kernel, nr, nc, parts),
        out_shape=(
            jax.ShapeDtypeStruct((rows, size), f32),
            jax.ShapeDtypeStruct((ratio, rows, size), f32),
            jax.ShapeDtypeStruct((8, BLK), f32),
        ),
        in_specs=[pl.BlockSpec(memory_space=pl.ANY)] + [vmem] * 4,
        out_specs=(vmem,) * 3,
        scratch_shapes=[
            pltpu.VMEM((rows, cols), f32),
            pltpu.VMEM((cols, size), jnp.bfloat16),
            pltpu.VMEM((cols, size), jnp.bfloat16),
            pltpu.VMEM((rows, size), f32),
            pltpu.VMEM((rows, size), f32),
            pltpu.VMEM((rows, size), f32),
            pltpu.VMEM((packed, BLK), f32),
            pltpu.VMEM((packed, BLK), f32),
            pltpu.VMEM((landing, BLK), f32),
            pltpu.VMEM((nc - 1, rows // nc, size), f32),
            pltpu.VMEM((size, 2 * size), f32),
            pltpu.VMEM((BLK, 2 * BLK), f32),
            pltpu.SemaphoreType.DMA((sems,)),
            pltpu.SemaphoreType.DMA((sems,)),
            pltpu.SemaphoreType.DMA((parts,)),
        ],
        compiler_params=pltpu.CompilerParams(collective_id=0, has_side_effects=True, vmem_limit_bytes=48 * 1024 * 1024),
    )(covariance, state, cells, weights, variance)


def dot(a, b, precision):
    return jnp.dot(a, b, precision=precision, preferred_element_type=jnp.float32)


def on_device(mesh, covariance, state_mean, obs_values, obs_cells, obs_weights, obs_variance):
    rows_dev, cols_dev = covariance.shape
    devices = mesh.shape["row"] * mesh.shape["col"]
    batches, foot, width = obs_cells.shape
    total = batches * width
    filled = len(pair_blocks(total)) * BLK + 8
    unit = 8 * devices
    packed = -(-(filled + 8) // unit) * unit
    u, cross_cols, pred = exchange(mesh, packed, covariance, state_mean.reshape(1, rows_dev), obs_cells, obs_weights, obs_variance)
    innov = obs_values.reshape(total) - pred[: total // BLK].reshape(total)
    mean = state_mean + jnp.sum(u * innov[None, :], axis=1)
    matrix = covariance - dot(u, cross_cols.reshape(cols_dev, total).T, MID)
    return (matrix, mean)


def solution(mesh):
    return jax.shard_map(
        functools.partial(on_device, mesh),
        mesh=mesh,
        in_specs=(P("row", "col"), P("row"), P(), P(), P(), P()),
        out_specs=(P("row", "col"), P("row")),
        check_vma=False,
    )
```

time: 131 us -> 109 us (0.83)
  matrix products: 23.9 us -> 11.1 us
  Pallas kernels: 100 us -> 91.6 us
    dot_general x3 -> x1, matrix products: 23.9 us -> 11.1 us  [dot(): jnp.dot(a, b, precision=precision, preferred_element_type=jnp.float32)]
    pallas_call x1, Pallas kernels: 100 us -> 91.6 us  [exchange(): pl.pallas_call(functools.partial(kernel, nr, nc, parts), out_shape=(jax.S...]
    unnamed x8 -> x11, local copies, waits for them, and re-layouts: 1.39 us -> 3.45 us
    slice x2 -> x0, local copies, waits for them, and re-layouts: 1.71 us -> none  [the longest x1 0.86 us: local_operator(): cells[foot][None, :] == positions]
where the time goes in v1:
time: 109 us; the launch traced here: 108 us
  Pallas kernels  91.6 us (84%)
  matrix products  11.1 us (10%)
  local copies, waits for them, and re-layouts  3.45 us (3%)
    pallas_call x1, Pallas kernels, exchange(): pl.pallas_call(functools.partial(kernel, nr, nc, parts), out_shape=(jax.S...  91.6 us
    dot_general x1, matrix products, dot(): jnp.dot(a, b, precision=precision, preferred_element_type=jnp.float32)  11.1 us
    unnamed x11, local copies, waits for them, and re-layouts  3.45 us

profile of v1, /device:TPU:7, one launch (start us, length us, event | category | flops | bytes accessed | tf_op | source)
XLA Modules:
  0.0 107.6 jit_solution(6389895946742110109)
XLA Ops:
  0.6 0.7 copy.8
  1.3 0.0 copy-start
  1.3 0.7 copy-done
  2.0 0.0 copy-start.1
  2.0 0.7 copy-done.1
  2.7 0.0 copy-start.2
  2.7 0.7 copy-done.2
  3.4 0.0 copy-start.3
  3.4 0.7 copy-done.3
  4.1 0.0 copy-start.4
  4.1 91.6 %shard_map.77 = (f32[1024,512]{1,0:T(8,128)S(1)}, f32[2,1024,512]{2,1,0:T(8,128)}, f32[8,128]{1,0:T(8,128)S(1)}) custom-call(f32[1024,2048]{1,0:T(8,128)} %p_ref.1, f32[1,1024]{1,0:T(1,128)S(1)} %bitcast.8, s32[2,4,256]{2,1,0:T(4,128)S(1)} %copy-done.1, f32[2,4,256]{2,1,0:T(4,128)S(1)} %copy-done.2, f32[2,256]{1,0:T(2,128)S(1)} %copy-done.3), custom_call_target="tpu_custom_call" | custom-call | tf_op jit(solution)/shard_map/pallas_call | solution.py:395
  95.7 0.2 multiply_reduce_fusion
  95.9 0.6 add.3
  96.5 0.0 copy-done.4
  96.5 11.1 %convolution_subtract_fusion = f32[1024,2048]{1,0:T(8,128)} fusion(f32[1024,2048]{1,0:T(8,128)S(1)} %copy-done.4, f32[1024,512]{1,0:T(8,128)S(1)} %get-tuple-element.5, f32[2048,512]{1,0:T(8,128)} %bitcast.9), kind=kOutput, calls=%fused_computation | convolution fusion | flops 6444548096 | bytes 23068672 | tf_op jit(solution)/shard_map/dot_general | solution.py:426
  (1 shorter events, 0.0 us)
Async XLA Ops:
  1.3 0.7 copy-start
  2.0 0.7 copy-start.1
  2.7 0.7 copy-start.2
  3.4 0.7 copy-start.3
  4.1 92.4 %copy-start.4 = (f32[1024,2048]{1,0:T(8,128)S(1)}, f32[1024,2048]{1,0:T(8,128)}, u32[]{:S(2)}) copy-start(f32[1024,2048]{1,0:T(8,128)} %p_ref.1) | copy-start | bytes 25165828

commit v2 on v1

v2 whole, which is shorter than its diff:
```python
import functools

import jax
import jax.numpy as jnp
from jax import lax
from jax.experimental import pallas as pl
from jax.experimental.pallas import tpu as pltpu
from jax.sharding import PartitionSpec as P

HI = lax.Precision.HIGHEST
MID = lax.Precision.HIGH
MESH = pl.DeviceIdType.MESH
BLK = 128
SUB = 8
PANEL = 32
UNITS = 4

def base_inverse(work, hook):
    tiles = PANEL // SUB

    def panel_step(first, g, carry):
        start = pl.multiple_of(g * PANEL, PANEL)
        panel = work[pl.ds(start, PANEL), :]
        square = pltpu.roll(panel[:, :BLK], BLK - start, 1)[:, :PANEL]
        rows = [slice(t * SUB, (t + 1) * SUB) for t in range(tiles)]
        wide = [[jnp.broadcast_to(square[rows[t], j : j + 1], (SUB, BLK)) for t in range(tiles)] for j in range(PANEL)]
        left = [panel[rows[t], :BLK] for t in range(tiles)]
        right = [panel[rows[t], BLK:] for t in range(tiles)]
        below = lax.broadcasted_iota(jnp.int32, (SUB, BLK), 0)
        scale = [jnp.zeros((SUB, BLK), jnp.float32) for t in range(tiles)]
        for j in range(PANEL):
            home, at = j // SUB, j % SUB
            line = slice(at, at + 1)
            pivot = jnp.broadcast_to(wide[j][home][line, :], (SUB, BLK))
            root = lax.rsqrt(pivot)
            scale[home] = jnp.where(below == at, root, scale[home])
            pivot_left, pivot_right = left[home][line, :], right[home][line, :]
            pivot_wide = [wide[k][home][line, :] for k in range(PANEL)]
            for t in range(home, tiles):
                ratio = wide[j][t] * (1.0 / pivot)
                if t == home:
                    ratio = jnp.where(below > at, ratio, 0.0)
                left[t] = left[t] - ratio * pivot_left
                right[t] = right[t] - ratio * pivot_right
                for k in range(j + 1, PANEL):
                    wide[k][t] = wide[k][t] - ratio * pivot_wide[k]
        left = jnp.concatenate([left[t] * scale[t] for t in range(tiles)], axis=0)
        right = jnp.concatenate([right[t] * scale[t] for t in range(tiles)], axis=0)
        both = jnp.concatenate([left, right], axis=1)
        lane = lax.broadcasted_iota(jnp.int32, (PANEL, BLK), 1)
        lhs = jnp.where(lane >= start + PANEL, left, 0.0)
        work[pl.ds(start, PANEL), :] = both
        work[first:, :] = work[first:, :] - lax.dot_general(lhs[:, first:], both, (((0,), (0,)), ((), ())), precision=HI, preferred_element_type=jnp.float32)
        return carry

    steps = BLK // PANEL // 4
    for quarter in range(4):
        hook(quarter)
        first = quarter * steps * PANEL
        lax.fori_loop(quarter * steps, (quarter + 1) * steps, functools.partial(panel_step, first), 0)


def factor_inverse(mat, work, hook, ready):
    size = mat.shape[0]
    eye = (lax.broadcasted_iota(jnp.int32, (BLK, BLK), 0) == lax.broadcasted_iota(jnp.int32, (BLK, BLK), 1)).astype(jnp.float32)
    for b in range(size // BLK):
        lo, hi = b * BLK, (b + 1) * BLK
        work[:, :BLK] = mat[lo:hi, lo:hi]
        work[:, BLK:] = eye
        base_inverse(work, lambda quarter: hook(4 * b + quarter))
        winv = work[:, BLK:]
        ready(b)
        if hi < size:
            panel = jnp.dot(winv, mat[lo:hi, hi:size], precision=HI, preferred_element_type=jnp.float32)
        if lo > 0:
            left = jnp.dot(winv, mat[lo:hi, size : size + lo], precision=HI, preferred_element_type=jnp.float32)
            mat[lo:hi, size : size + lo] = left
        mat[lo:hi, size + lo : size + hi] = winv
        if hi < size:
            right = mat[lo:hi, size : size + hi]
            dims = (((0,), (0,)), ((), ()))
            mat[hi:size, hi:size] = mat[hi:size, hi:size] - lax.dot_general(panel, panel, dims, precision=HI, preferred_element_type=jnp.float32)
            mat[hi:size, size : size + hi] = mat[hi:size, size : size + hi] - lax.dot_general(panel, right, dims, precision=HI, preferred_element_type=jnp.float32)


def pair_blocks(size):
    count = size // BLK
    return [(i, j) for i in range(count) for j in range(i + 1)]


def split(value):
    high = value.astype(jnp.bfloat16)
    return high, (value - high.astype(jnp.float32)).astype(jnp.bfloat16)


def matmul(a, b, dims=(((1,), (0,)), ((), ()))):
    return lax.dot_general(a, b, dims, preferred_element_type=jnp.float32)


def part_count(rows, nc):
    return 4 if rows % (4 * nc * SUB) == 0 else 2


def plane_shape(nc):
    flat = max(d for d in range(1, nc + 1) if nc % d == 0 and d * d <= nc)
    return nc // flat, flat


def relay_order(nc, parts):
    order = []
    for pair in range(0, parts, 2):
        order += [(0, pair), (0, pair + 1)]
        order += [(d, h) for h in (pair, pair + 1) for d in range(1, nc)]
    return order


def kernel(
    nr, nc, parts, batches, foot, p_ref, pack_ref, u_out, xc_ref, innov_ref,
    u_ref, keep_sem, block, high_op, low_op, row_op, t_ref, xr_ref, acc0, full0, land0, acc1, full1, land1,
    tland, land_a, land_b, mid_a, mid_b, next_a, next_b, mat, work, send_sem, recv_sem, load_sem,
):
    ratio = nr // nc
    row, col = lax.axis_index("row"), lax.axis_index("col")
    high, low = row // ratio, row % ratio
    rows, size = t_ref.shape
    wide = block.shape[1]
    part = rows // parts
    sub = part // nc
    order = relay_order(nc, parts)
    pieces = len(order)
    used = [0]

    def take(count):
        used[0] += count
        return used[0] - count

    width = pack_ref.shape[1]
    listed = batches * foot
    var_row, value_row, state_row = 2 * listed, 2 * listed + batches, 2 * listed + 2 * batches
    loads = []
    for h in range(parts):
        where = pl.ds(h * part, part)
        loads.append(pltpu.make_async_copy(p_ref.at[where], block.at[where], load_sem.at[h]))
        loads[-1].start()

    levels = [
        (ratio, low, lambda d: (high * ratio + lax.rem(low + d, ratio), col)),
        (nc, col, lambda d: (row, lax.rem(col + d, nc))),
        (nc, high, lambda d: (lax.rem(high + d, nc) * ratio + low, col)),
    ]
    barrier = pltpu.get_barrier_semaphore()
    for n, me, peer in levels:
        for d in range(1, n):
            pl.semaphore_signal(barrier, inc=1, device_id=peer(d), device_id_type=MESH)

    def operator(first, count, store):
        step = min(count, BLK)

        def fill(g, carry):
            start = pl.multiple_of(g * step, step)
            place = (lax.broadcasted_iota(jnp.int32, (step, width), 0) + (first + start)).astype(jnp.float32)
            for b in range(batches):
                total = jnp.zeros((step, width), jnp.float32)
                for f in range(foot):
                    at = b * foot + f
                    weight = pack_ref[listed + at : listed + at + 1, :]
                    total = total + jnp.where(pack_ref[at : at + 1, :] == place, weight, 0.0)
                store(start, step, b * width, width, total)
            return carry

        lax.fori_loop(0, count // step, fill, 0)

    def store_col(start, step, lane, width, total):
        h, l = split(total)
        high_op[pl.ds(start, step), lane : lane + width] = h
        low_op[pl.ds(start, step), lane : lane + width] = l

    def store_row(start, step, lane, width, total):
        row_op[pl.ds(start, step), lane : lane + width] = total

    operator(col * wide, wide, store_col)

    def remote(src, dst, sem, device):
        return pltpu.make_async_remote_copy(
            src_ref=src, dst_ref=dst, send_sem=send_sem.at[sem], recv_sem=recv_sem.at[sem],
            device_id=device, device_id_type=MESH,
        )

    def own_rows(h, owner):
        return pl.ds(pl.multiple_of(h * part + owner * sub, 8), sub)

    _, _, col_peer = levels[1]
    _, _, low_peer = levels[0]
    tall, flat = plane_shape(nc)
    hi, lo = col // flat, col % flat
    half = size // 2
    left, right = pl.ds(0, half), pl.ds(half, half)
    chain_base = take(pieces)
    sib_base = take(ratio - 1)
    up_sem, down_sem = sib_base + ratio - 1, sib_base + ratio
    take(2)

    def lo_peer(d):
        return (row, hi * flat + lax.rem(lo + d, flat))

    def hi_peer(d):
        return (row, lax.rem(hi + d, tall) * flat + lo)

    def plane_copies(h):
        stages = scatter, settle, spread, pass_on = [], [], [], []
        base = take(len(stages))

        def add(group, src, dst, device):
            stage = [n for n in range(len(stages)) if stages[n] is group][0]
            group.append(remote(src, dst, base + stage, device))

        own = own_rows(h, col)
        for d in range(1, flat):
            other = lax.rem(lo + d, flat)
            for k in range(tall):
                add(scatter, t_ref.at[own_rows(h, k * flat + other), left], land_a.at[h, d - 1, k], lo_peer(d))
            add(settle, mid_b.at[h, other], next_b.at[h, d - 1], lo_peer(d))
            add(spread, xr_ref.at[own, left], xr_ref.at[own, left], lo_peer(d))
            for k in range(tall):
                where = own_rows(h, k * flat + lo)
                add(pass_on, xr_ref.at[where, right], xr_ref.at[where, right], lo_peer(d))
        for d in range(1, tall):
            other = lax.rem(hi + d, tall)
            for k in range(flat):
                add(scatter, t_ref.at[own_rows(h, other * flat + k), right], land_b.at[h, d - 1, k], hi_peer(d))
            add(settle, mid_a.at[h, other], next_a.at[h, d - 1], hi_peer(d))
            add(spread, xr_ref.at[own, right], xr_ref.at[own, right], hi_peer(d))
            for k in range(flat):
                where = own_rows(h, hi * flat + k)
                add(pass_on, xr_ref.at[where, left], xr_ref.at[where, left], hi_peer(d))
        near = (flat - 1) + (tall - 1)
        wide_count = (flat - 1) * tall + (tall - 1) * flat
        ends = []
        for stage, count in enumerate((wide_count, near, near, wide_count)):
            every = tland.at[pl.ds(0, count * sub // 2)]
            ends.append(remote(every, every, base + stage, lo_peer(1)))
        return stages, ends

    plane = [plane_copies(h) for h in range(parts)]

    def start_all(copies):
        for copy in copies:
            copy.start()

    def scatter(h):
        start_all(plane[h][0][0])

    def settle(h):
        plane[h][1][0].wait()
        for k in range(tall):
            total = t_ref[own_rows(h, k * flat + lo), left]
            for d in range(1, flat):
                total = total + land_a[h, d - 1, k]
            mid_a[h, k] = total
        for k in range(flat):
            total = t_ref[own_rows(h, hi * flat + k), right]
            for d in range(1, tall):
                total = total + land_b[h, d - 1, k]
            mid_b[h, k] = total
        start_all(plane[h][0][1])

    def spread(h):
        plane[h][1][1].wait()
        total = mid_a[h, hi]
        for d in range(1, tall):
            total = total + next_a[h, d - 1]
        xr_ref[own_rows(h, col), left] = total
        total = mid_b[h, lo]
        for d in range(1, flat):
            total = total + next_b[h, d - 1]
        xr_ref[own_rows(h, col), right] = total
        start_all(plane[h][0][2])

    def pass_on(h):
        plane[h][1][2].wait()
        start_all(plane[h][0][3])

    def arrive(h):
        plane[h][1][3].wait_recv()

    source = high == col
    far = jnp.abs(high - col)
    top = nc - 1
    above = (jnp.minimum(high + 1, top) * ratio + low, col)
    below = (jnp.maximum(high - 1, 0) * ratio + low, col)
    goes_up = jnp.logical_and(high >= col, high < top)
    goes_down = jnp.logical_and(high <= col, high > 0)

    def onward(where, src, e):
        dst = xc_ref.at[low, where]
        up = pltpu.make_async_remote_copy(
            src_ref=src, dst_ref=dst, send_sem=send_sem.at[up_sem], recv_sem=recv_sem.at[chain_base + e],
            device_id=above, device_id_type=MESH,
        )
        down = pltpu.make_async_remote_copy(
            src_ref=src, dst_ref=dst, send_sem=send_sem.at[down_sem], recv_sem=recv_sem.at[chain_base + e],
            device_id=below, device_id_type=MESH,
        )
        sibs = [remote(src, dst, sib_base + q - 1, low_peer(q)) for q in range(1, ratio)]
        return up, down, sibs

    def links(e, src_is_own):
        d, h = order[e]
        where = own_rows(h, lax.rem(col - d + nc, nc))
        src = xr_ref.at[where] if src_is_own else xc_ref.at[low, where]
        return (where,) + onward(where, src, e)

    def send_on(up, down, sibs):
        @pl.when(goes_up)
        def _():
            up.start()

        @pl.when(goes_down)
        def _():
            down.start()

        for sib in sibs:
            sib.start()

    def keep(e):
        d, h = order[e]
        where = own_rows(h, lax.rem(col - d + nc, nc))
        return pltpu.make_async_copy(xr_ref.at[where], xc_ref.at[low, where], keep_sem.at[0])

    def relay_source(e):
        d, h = order[e]
        where, up, down, sibs = links(e, True)
        send_on(up, down, sibs)
        keep(e).start()

    def relay(e):
        where, up, down, sibs = links(e, False)
        up.wait_recv()
        send_on(up, down, sibs)

    def emit(pieces_now):
        @pl.when(source)
        def _():
            for e in pieces_now:
                relay_source(e)

    def group(h):
        return [e for e in range(pieces) if order[e][1] == h and order[e][0] > 0]

    def own(h):
        return [order.index((0, h))]

    def point(k):
        for test, lag in ((far == 1, 0), (far == 2, 2), (far > 2, 4)):
            if 0 <= k - lag < pieces:
                pl.when(test)(functools.partial(relay, k - lag))

    for h in range(parts):
        loads[h].wait()
        where = slice(h * part, (h + 1) * part)
        a, b = split(block[where, :])
        t_ref[where, :] = matmul(a, high_op[...]) + matmul(a, low_op[...]) + matmul(b, high_op[...])
        if h == 0:
            pl.semaphore_wait(barrier, ratio - 1 + 2 * (nc - 1))
        if h < 2:
            scatter(h)
        if h == parts - 2:
            operator(row * rows, rows, store_row)

    def reduced(acc, full, land, spread):
        start, length, slot = 0, acc.shape[0], 0
        spots = []

        def exchange_all(level, pairs, count):
            n, me, peer = levels[level]
            base = take(1)
            for d in range(1, n):
                src, dst = pairs(d)
                remote(src, dst, base, peer(d)).start()
            every = land.at[pl.ds(0, (n - 1) * count)]
            return remote(every, every, base, peer(1))

        for level, (n, me, peer) in enumerate(levels):
            whole = level == 2 and not spread
            segment = length if whole else length // n

            def scattered(d):
                begin = start if whole else pl.multiple_of(start + lax.rem(me + d, n) * segment, 8)
                return acc.at[pl.ds(begin, segment)], land.at[pl.ds(slot + (d - 1) * segment, segment)]

            end = exchange_all(level, scattered, segment)
            yield
            if not whole:
                start = pl.multiple_of(start + me * segment, 8)
                spots.append((start, segment))
            length = segment
            end.wait()
            where = pl.ds(start, length)
            mine = acc[where, :]
            for d in range(1, n):
                mine = mine + land[pl.ds(slot + (d - 1) * segment, segment), :]
            slot += (n - 1) * segment
            if level == 2:
                full[where, :] = mine
            else:
                acc[where, :] = mine
        for level in (2, 1, 0) if spread else (1, 0):
            begin, segment = spots[level]
            where = full.at[pl.ds(begin, segment)]
            end = exchange_all(level, lambda d: (where, where), segment)
            yield
            end.wait()
        yield

    def sums(i):
        return lax.dot_general(
            row_op[:, i * BLK : (i + 1) * BLK], t_ref[:, : (i + 1) * BLK], (((0,), (0,)), ((), ())),
            precision=MID, preferred_element_type=jnp.float32,
        )

    first = reduced(acc0, full0, land0, False)
    rest = reduced(acc1, full1, land1, True)
    place = 0
    settle(0)
    for i in range(size // BLK):
        blocks = sums(i)
        if i == 0:
            acc0[:BLK, :] = blocks
            if acc0.shape[0] > BLK:
                acc0[BLK:, :] = jnp.zeros((acc0.shape[0] - BLK, BLK), jnp.float32)
            next(first)
            continue
        for j in range(i + 1):
            acc1[place : place + BLK, :] = blocks[:, j * BLK : (j + 1) * BLK]
            place += BLK
        if i == 1:
            next(first)
            settle(1)
        if i == 2:
            spread(0)
            next(first)
            emit(own(0))
    predicted = jnp.zeros((1, size), jnp.float32)
    for q in range(rows // width):
        state = pack_ref[state_row + q : state_row + q + 1, :]
        predicted = predicted + jnp.dot(
            state, row_op[q * width : (q + 1) * width, :], precision=HI, preferred_element_type=jnp.float32
        )
    predicted = jnp.where(col == 0, predicted, 0.0)
    acc1[place:, :] = jnp.zeros((acc1.shape[0] - place, BLK), jnp.float32)
    for i in range(size // BLK):
        acc1[place + i : place + i + 1, :] = predicted[:, i * BLK : (i + 1) * BLK]
    next(rest)
    spread(1)
    pass_on(0)
    emit(own(1))
    next(first)
    next(rest)
    pass_on(1)
    arrive(0)
    emit(group(0)[:1])
    next(first)
    point(0)
    next(first)
    next(rest)
    emit(group(0)[1:])
    if parts > 2:
        scatter(2)
    point(1)

    same = lax.broadcasted_iota(jnp.int32, (BLK, BLK), 0) == lax.broadcasted_iota(jnp.int32, (BLK, BLK), 1)

    def place_block(i, j, square):
        if i == j:
            lane = i * BLK % width
            line = var_row + i * BLK // width
            diagonal = pack_ref[line : line + 1, lane : lane + BLK]
            square = 0.5 * (square + square.T) + jnp.where(same, diagonal, 0.0)
        mat[i * BLK : (i + 1) * BLK, j * BLK : (j + 1) * BLK] = square
        if i != j:
            mat[j * BLK : (j + 1) * BLK, i * BLK : (i + 1) * BLK] = square.T

    place_block(0, 0, full0[:BLK, :])
    mat[:, size:] = jnp.zeros((size, size), jnp.float32)

    points = {2: 2, 4: 6, 6: 7, 7: 8, 8: 9, 10: 10, 12: 11, 14: 12}

    def hook(slot):
        if slot == 1:
            next(rest)
        if slot == 3:
            arrive(1)
            emit(group(1))
        if parts > 2:
            if slot == 2:
                scatter(3)
            if slot == 3:
                settle(2)
            if slot == 5:
                spread(3)
                emit(own(3))
                pass_on(2)
            if slot == 7:
                pass_on(3)
                arrive(2)
                emit(group(2))
            if slot == 10:
                arrive(3)
                emit(group(3))
        if slot in points:
            point(points[slot])

    def ready(b):
        if b == 0:
            next(rest)
            point(3)
            next(rest)
            if parts > 2:
                spread(2)
                emit(own(2))
                settle(3)
            point(4)
            next(rest)
            point(5)
            for index, (i, j) in enumerate(pair_blocks(size)[1:]):
                place_block(i, j, full1[index * BLK : (index + 1) * BLK, :])
            innov_ref[...] = jnp.zeros((8, BLK), jnp.float32)
            for i in range(size // BLK):
                lane = i * BLK % width
                line = value_row + i * BLK // width
                value = pack_ref[line : line + 1, lane : lane + BLK]
                innov_ref[i : i + 1, :] = value - full1[place + i : place + i + 1, :]

    factor_inverse(mat, work, hook, ready)
    done = [13]

    def advance(last):
        while done[0] <= last:
            point(done[0])
            done[0] += 1

    advance(13)
    middle = size // 2
    across, along = (((1,), (1,)), ((), ())), (((1,), (0,)), ((), ()))
    high_w, low_w = split(mat[:, size:])

    def product(value, rows_w, lanes_w, dims):
        a, b = split(value)
        c, d = high_w[rows_w, lanes_w], low_w[rows_w, lanes_w]
        return matmul(a, c, dims) + matmul(a, d, dims) + matmul(b, c, dims)

    lower, upper, every = slice(0, middle), slice(middle, size), slice(0, size)
    step = rows // UNITS
    results = []
    for c in range(UNITS):
        where = slice(c * step, (c + 1) * step)
        gain_left = product(xr_ref[where, lower], lower, lower, across)
        gain_right = product(xr_ref[where, :], upper, every, across)
        u_ref[where, lower] = product(jnp.concatenate([gain_left, gain_right], axis=1), every, lower, along)
        u_ref[where, upper] = product(gain_right, upper, upper, along)
        results.append(pltpu.make_async_copy(u_ref.at[pl.ds(c * step, step)], u_out.at[pl.ds(c * step, step)], keep_sem.at[1]))
        results[-1].start()
        if c % 2 == 1:
            advance(done[0])
    advance(pieces + 3)
    pltpu.make_async_copy(u_ref, u_out, keep_sem.at[1]).wait()
    everything = pl.ds(0, rows)

    @pl.when(source)
    def _():
        pltpu.make_async_copy(xr_ref, xc_ref.at[low], keep_sem.at[0]).wait()

    for h in range(parts):
        plane[h][1][3].wait_send()
    up, down, sibs = onward(everything, xr_ref, 0)

    @pl.when(goes_up)
    def _():
        up.wait_send()

    @pl.when(goes_down)
    def _():
        down.wait_send()

    for sib in sibs:
        sib.wait()


def padded(count, unit):
    return -(-count // unit) * unit


def exchange(mesh, covariance, pack, batches, foot):
    nr, nc = mesh.shape["row"], mesh.shape["col"]
    ratio = nr // nc
    rows, cols = covariance.shape
    size = batches * pack.shape[1]
    parts = part_count(rows, nc)
    group = ratio * nc
    lead = padded(BLK, 8 * group)
    follow = padded((len(pair_blocks(size)) - 1) * BLK + 8, 8 * group * nc)
    half, quarter = follow // ratio, follow // group
    land0 = (ratio - 1) * (lead // ratio) + 2 * (nc - 1) * (lead // group)
    land1 = (ratio - 1) * half + (nc - 1) * quarter + (nc - 1) * (quarter // nc)
    tall, flat = plane_shape(nc)
    sub = rows // (parts * nc)
    pieces = nc * parts
    sems = 2 * 2 * 3 + 4 * parts + pieces + ratio + 1
    f32 = jnp.float32
    vmem = pl.BlockSpec(memory_space=pltpu.VMEM)
    return pl.pallas_call(
        functools.partial(kernel, nr, nc, parts, batches, foot),
        out_shape=(
            jax.ShapeDtypeStruct((rows, size), f32),
            jax.ShapeDtypeStruct((ratio, rows, size), f32),
            jax.ShapeDtypeStruct((8, BLK), f32),
        ),
        in_specs=[pl.BlockSpec(memory_space=pl.ANY), vmem],
        out_specs=(pl.BlockSpec(memory_space=pl.ANY),) * 2 + (vmem,),
        scratch_shapes=[
            pltpu.VMEM((rows, size), f32),
            pltpu.SemaphoreType.DMA((2,)),
            pltpu.VMEM((rows, cols), f32),
            pltpu.VMEM((cols, size), jnp.bfloat16),
            pltpu.VMEM((cols, size), jnp.bfloat16),
            pltpu.VMEM((rows, size), f32),
            pltpu.VMEM((rows, size), f32),
            pltpu.VMEM((rows, size), f32),
            pltpu.VMEM((lead, BLK), f32),
            pltpu.VMEM((lead, BLK), f32),
            pltpu.VMEM((land0, BLK), f32),
            pltpu.VMEM((follow, BLK), f32),
            pltpu.VMEM((follow, BLK), f32),
            pltpu.VMEM((land1, BLK), f32),
            pltpu.VMEM(((flat - 1) * tall * sub, size), f32),
            pltpu.VMEM((parts, flat - 1, tall, sub, size // 2), f32),
            pltpu.VMEM((parts, tall - 1, flat, sub, size // 2), f32),
            pltpu.VMEM((parts, tall, sub, size // 2), f32),
            pltpu.VMEM((parts, flat, sub, size // 2), f32),
            pltpu.VMEM((parts, tall - 1, sub, size // 2), f32),
            pltpu.VMEM((parts, flat - 1, sub, size // 2), f32),
            pltpu.VMEM((size, 2 * size), f32),
            pltpu.VMEM((BLK, 2 * BLK), f32),
            pltpu.SemaphoreType.DMA((sems,)),
            pltpu.SemaphoreType.DMA((sems,)),
            pltpu.SemaphoreType.DMA((parts,)),
        ],
        compiler_params=pltpu.CompilerParams(collective_id=0, has_side_effects=True, vmem_limit_bytes=40 * 1024 * 1024),
    )(covariance, pack)


def on_device(mesh, covariance, state_mean, obs_values, obs_cells, obs_weights, obs_variance):
    rows_dev, cols_dev = covariance.shape
    batches, foot, width = obs_cells.shape
    total = batches * width
    pack = jnp.concatenate(
        [
            obs_cells.astype(jnp.float32).reshape(batches * foot, width),
            obs_weights.reshape(batches * foot, width),
            obs_variance,
            obs_values,
            state_mean.reshape(rows_dev // width, width),
        ],
        axis=0,
    )
    u, cross_cols, innov = exchange(mesh, covariance, pack, batches, foot)
    innov = innov[: total // BLK].reshape(total)
    mean = state_mean + jnp.sum(u * innov[None, :], axis=1)
    update = jnp.dot(u, cross_cols.reshape(cols_dev, total).T, precision=MID, preferred_element_type=jnp.float32)
    return (covariance - update, mean)


def solution(mesh):
    return jax.shard_map(
        functools.partial(on_device, mesh),
        mesh=mesh,
        in_specs=(P("row", "col"), P("row"), P(), P(), P(), P()),
        out_specs=(P("row", "col"), P("row")),
        check_vma=False,
    )
```

time: 109 us -> 102 us (0.936); the launches traced: 108 us -> 102 us
  Pallas kernels: 91.6 us -> 88 us
  matrix products: 11.1 us -> 9.57 us
  local copies, waits for them, and re-layouts: 3.45 us -> 2.14 us
    pallas_call x1, Pallas kernels: 91.6 us -> 88 us  [exchange(): pl.pallas_call(functools.partial(kernel, nr, nc, parts, batches, foot), o...]
    unnamed x11 -> x4, local copies, waits for them, and re-layouts: 3.45 us -> 0.01 us
    dot_general x1, matrix products: 11.1 us -> 9.57 us  [on_device(): jnp.dot(u, cross_cols.reshape(cols_dev, total).T, precision=MID, preferre...]
    reshape x0 -> x3, local copies, waits for them, and re-layouts: none -> 1.41 us  [the longest x1 0.7 us: on_device(): obs_weights.reshape(batches * foot, width)]
where the time goes in v2:
time: 102 us
  Pallas kernels  88 us (86%)
  matrix products  9.57 us (9%)
  local copies, waits for them, and re-layouts  2.14 us (2%)
  other arithmetic  1.51 us (1%)
    pallas_call x1, Pallas kernels, exchange(): pl.pallas_call(functools.partial(kernel, nr, nc, parts, batches, foot), o...  88 us
    dot_general x1, matrix products, on_device(): jnp.dot(u, cross_cols.reshape(cols_dev, total).T, precision=MID, preferre...  9.57 us

profile of v2, /device:TPU:7, one launch (start us, length us, event | category | flops | bytes accessed | tf_op | source)
XLA Modules:
  0.0 101.9 jit_solution(7657992122088810362)
XLA Ops:
  0.6 0.7 reshape.19
  1.3 0.7 convert_element_type.3
  2.0 0.7 reshape.18
  2.7 0.7 concatenate.3.pack_ref
  3.5 0.0 copy-start.1
  3.5 0.0 copy-start
  3.5 88.0 %shard_map.77 = (f32[1024,512]{1,0:T(8,128)S(1)}, f32[2,1024,512]{2,1,0:T(8,128)S(1)}, f32[8,128]{1,0:T(8,128)S(1)}) custom-call(f32[1024,2048]{1,0:T(8,128)} %p_ref.1, f32[24,256]{1,0:T(8,128)S(1)} %concatenate.3.pack_ref), custom_call_target="tpu_custom_call" | custom-call | tf_op jit(solution)/shard_map/pallas_call | solution.py:611
  91.5 0.2 multiply_reduce_fusion
  91.8 0.0 copy-done.1
  91.8 0.6 add.3
  92.4 0.0 copy-done
  92.4 9.6 %convolution_subtract_fusion = f32[1024,2048]{1,0:T(8,128)} fusion(f32[1024,2048]{1,0:T(8,128)S(1)} %copy-done, f32[1024,512]{1,0:T(8,128)S(1)} %get-tuple-element.5, f32[2048,512]{1,0:T(8,128)S(1)} %bitcast.5), kind=kOutput, calls=%fused_computation | convolution fusion | flops 6444548096 | bytes 23068672 | tf_op jit(solution)/shard_map/dot_general | solution.py:669
  (2 shorter events, 0.0 us)
Async XLA Ops:
  3.5 88.3 %copy-start.1 = (f32[1024]{0:T(1024)S(1)}, f32[1024]{0:T(1024)}, u32[]{:S(2)}) copy-start(f32[1024]{0:T(1024)} %param.7) | copy-start | bytes 12292
  3.5 88.9 %copy-start = (f32[1024,2048]{1,0:T(8,128)S(1)}, f32[1024,2048]{1,0:T(8,128)}, u32[]{:S(2)}) copy-start(f32[1024,2048]{1,0:T(8,128)} %p_ref.1) | copy-start | bytes 25165828

commit v3 on v2

--- a/solution.py
+++ b/solution.py
@@ -13,7 +13,7 @@
 BLK = 128
 SUB = 8
 PANEL = 32
-UNITS = 4
+UNITS = 2
 
 def base_inverse(work, hook):
     tiles = PANEL // SUB
@@ -117,7 +117,7 @@
 def kernel(
     nr, nc, parts, batches, foot, p_ref, pack_ref, u_out, xc_ref, innov_ref,
     u_ref, keep_sem, block, high_op, low_op, row_op, t_ref, xr_ref, acc0, full0, land0, acc1, full1, land1,
-    tland, land_a, land_b, mid_a, mid_b, next_a, next_b, mat, work, send_sem, recv_sem, load_sem,
+    side_ref, tland, land_a, land_b, mid_a, mid_b, next_a, next_b, mat, work, send_sem, recv_sem, load_sem,
 ):
     ratio = nr // nc
     row, col = lax.axis_index("row"), lax.axis_index("col")
@@ -310,12 +310,14 @@
         src = xr_ref.at[where] if src_is_own else xc_ref.at[low, where]
         return (where,) + onward(where, src, e)
 
-    def send_on(up, down, sibs):
-        @pl.when(goes_up)
+    def send_on(e, up, down, sibs):
+        owner = lax.rem(col - order[e][0] + nc, nc)
+
+        @pl.when(jnp.logical_and(goes_up, owner != top))
         def _():
             up.start()
 
-        @pl.when(goes_down)
+        @pl.when(jnp.logical_and(goes_down, owner != 0))
         def _():
             down.start()
 
@@ -330,13 +332,91 @@
     def relay_source(e):
         d, h = order[e]
         where, up, down, sibs = links(e, True)
-        send_on(up, down, sibs)
+        send_on(e, up, down, sibs)
         keep(e).start()
 
     def relay(e):
         where, up, down, sibs = links(e, False)
         up.wait_recv()
-        send_on(up, down, sibs)
+        send_on(e, up, down, sibs)
+
+    side_recv = take(nc * parts)
+    side_send = take(2 * nc)
+    last_up = jnp.logical_and(col == top, high < top)
+    last_down = jnp.logical_and(col == 0, high > 0)
+
+    def side(src, slot, h, lag, device):
+        dst = side_ref.at[slot, pl.ds(h * sub, sub)]
+        return pltpu.make_async_remote_copy(
+            src_ref=src, dst_ref=dst, send_sem=send_sem.at[side_send + lag],
+            recv_sem=recv_sem.at[side_recv + slot * parts + h], device_id=device, device_id_type=MESH,
+        )
+
+    def deliver(slot, h, lag, upward):
+        first = (h // 2) * 2 * nc + 2 + (h % 2) * (nc - 1)
+        e = first + (slot if upward else slot - 1)
+        return pltpu.make_async_remote_copy(
+            src_ref=side_ref.at[slot, pl.ds(h * sub, sub)], dst_ref=xc_ref.at[low, own_rows(h, top if upward else 0)],
+            send_sem=send_sem.at[side_send + nc + lag], recv_sem=recv_sem.at[chain_base + e],
+            device_id=(row, slot), device_id_type=MESH,
+        )
+
+    def side_start(h):
+        for test, device in ((last_up, above), (last_down, below)):
+            @pl.when(test)
+            def _():
+                side(xr_ref.at[own_rows(h, col)], high, h, 0, device).start()
+
+    def side_edges(lag):
+        up, down = high - lag, high + lag
+        return (
+            (True, up, jnp.logical_and(col == top, up >= 0), above, high < top),
+            (False, down, jnp.logical_and(col == 0, down <= top), below, high > 0),
+        )
+
+    def side_forward(h, lag):
+        for _, slot, edge, device, onward_too in side_edges(lag):
+            @pl.when(edge)
+            def _():
+                copy = side(side_ref.at[slot, pl.ds(h * sub, sub)], slot, h, lag, device)
+                copy.wait_recv()
+                pl.when(onward_too)(copy.start)
+
+    def side_deliver(h, lag):
+        for upward, slot, edge, _, _ in side_edges(lag):
+            pl.when(edge)(deliver(slot, h, lag, upward).start)
+
+    def each_lag(act, h, lag):
+        for each in range(lag, nc if lag == 3 else min(lag + 1, nc)):
+            act(h, each)
+
+    def side_take(h):
+        @pl.when(jnp.logical_not(source))
+        def _():
+            e = (h // 2) * 2 * nc + 2 + (h % 2) * (nc - 1) + jnp.where(high > col, col, col - 1)
+            where = own_rows(h, jnp.where(high > col, top, 0))
+            up, _, sibs = onward(where, xc_ref.at[low, where], e)
+            up.wait_recv()
+            for sib in sibs:
+                sib.start()
+
+    def side_drain():
+        span = pl.ds(0, parts * sub)
+        for upward in (True, False):
+            for lag in range(nc):
+                slot = high - lag if upward else high + lag
+                edge = jnp.logical_and(col == top, slot >= 0) if upward else jnp.logical_and(col == 0, slot <= top)
+                whole = pltpu.make_async_remote_copy(
+                    src_ref=tland.at[span], dst_ref=tland.at[span], send_sem=send_sem.at[side_send + lag],
+                    recv_sem=recv_sem.at[side_recv], device_id=above, device_id_type=MESH,
+                )
+                pl.when(jnp.logical_and(edge, high < top if upward else high > 0))(whole.wait_send)
+                if lag > 0:
+                    whole = pltpu.make_async_remote_copy(
+                        src_ref=tland.at[span], dst_ref=tland.at[span], send_sem=send_sem.at[side_send + nc + lag],
+                        recv_sem=recv_sem.at[side_recv], device_id=above, device_id_type=MESH,
+                    )
+                    pl.when(edge)(whole.wait_send)
 
     def emit(pieces_now):
         @pl.when(source)
@@ -353,7 +433,9 @@
     def point(k):
         for test, lag in ((far == 1, 0), (far == 2, 2), (far > 2, 4)):
             if 0 <= k - lag < pieces:
-                pl.when(test)(functools.partial(relay, k - lag))
+                owner = lax.rem(col - order[k - lag][0] + nc, nc)
+                chained = owner != jnp.where(high > col, top, 0)
+                pl.when(jnp.logical_and(test, chained))(functools.partial(relay, k - lag))
 
     for h in range(parts):
         loads[h].wait()
@@ -440,6 +522,7 @@
             spread(0)
             next(first)
             emit(own(0))
+            side_start(0)
     predicted = jnp.zeros((1, size), jnp.float32)
     for q in range(rows // width):
         state = pack_ref[state_row + q : state_row + q + 1, :]
@@ -452,20 +535,21 @@
         acc1[place + i : place + i + 1, :] = predicted[:, i * BLK : (i + 1) * BLK]
     next(rest)
     spread(1)
+    side_start(1)
     pass_on(0)
     emit(own(1))
     next(first)
     next(rest)
     pass_on(1)
-    arrive(0)
-    emit(group(0)[:1])
     next(first)
     point(0)
     next(first)
     next(rest)
-    emit(group(0)[1:])
+    arrive(0)
+    emit(group(0)[:1])
     if parts > 2:
         scatter(2)
+        scatter(3)
     point(1)
 
     same = lax.broadcasted_iota(jnp.int32, (BLK, BLK), 0) == lax.broadcasted_iota(jnp.int32, (BLK, BLK), 1)
@@ -483,30 +567,47 @@
     place_block(0, 0, full0[:BLK, :])
     mat[:, size:] = jnp.zeros((size, size), jnp.float32)
 
-    points = {2: 2, 4: 6, 6: 7, 7: 8, 8: 9, 10: 10, 12: 11, 14: 12}
+    points = {2: 2, 4: 6, 5: 7, 6: 8, 7: 9, 8: 10, 10: 11, 11: 12, 12: 13, 13: 14, 15: 15}
+
+    sides = {
+        4: [(side_forward, 0, 2), (side_forward, 1, 2)],
+        6: [(side_forward, 2, 1), (side_deliver, 0, 1), (side_deliver, 1, 1)],
+        7: [(side_forward, 3, 1)],
+        8: [(side_deliver, 0, 2), (side_deliver, 1, 2), (side_forward, 0, 3), (side_forward, 1, 3), (side_deliver, 0, 3), (side_deliver, 1, 3)],
+        9: [(side_forward, 2, 2), (side_deliver, 2, 1), (side_deliver, 3, 1)],
+        11: [(side_forward, 3, 2)],
+        12: [(side_deliver, 2, 2), (side_deliver, 3, 2)],
+        14: [(side_forward, 2, 3), (side_deliver, 2, 3)],
+        15: [(side_forward, 3, 3), (side_deliver, 3, 3)],
+    }
 
     def hook(slot):
         if slot == 1:
             next(rest)
+            emit(group(0)[1:])
+            for h in range(2):
+                each_lag(side_forward, h, 1)
+        if parts > 2 and slot == 2:
+            settle(2)
         if slot == 3:
             arrive(1)
             emit(group(1))
         if parts > 2:
-            if slot == 2:
-                scatter(3)
             if slot == 3:
-                settle(2)
+                settle(3)
+            if slot == 4:
+                pass_on(2)
             if slot == 5:
-                spread(3)
-                emit(own(3))
-                pass_on(2)
+                pass_on(3)
             if slot == 7:
-                pass_on(3)
                 arrive(2)
                 emit(group(2))
-            if slot == 10:
+            if slot == 9:
                 arrive(3)
                 emit(group(3))
+        for act, h, lag in sides.get(slot, ()):
+            if h < parts:
+                each_lag(act, h, lag)
         if slot in points:
             point(points[slot])
 
@@ -514,11 +615,15 @@
         if b == 0:
             next(rest)
             point(3)
+            if parts > 2:
+                spread(2)
+                side_start(2)
+                emit(own(2))
             next(rest)
             if parts > 2:
-                spread(2)
-                emit(own(2))
-                settle(3)
+                spread(3)
+                side_start(3)
+                emit(own(3))
             point(4)
             next(rest)
             point(5)
@@ -532,14 +637,14 @@
                 innov_ref[i : i + 1, :] = value - full1[place + i : place + i + 1, :]
 
     factor_inverse(mat, work, hook, ready)
-    done = [13]
+    done = [16]
 
     def advance(last):
         while done[0] <= last:
             point(done[0])
             done[0] += 1
 
-    advance(13)
+    advance(16)
     middle = size // 2
     across, along = (((1,), (1,)), ((), ())), (((1,), (0,)), ((), ()))
     high_w, low_w = split(mat[:, size:])
@@ -560,8 +665,9 @@
         u_ref[where, upper] = product(gain_right, upper, upper, along)
         results.append(pltpu.make_async_copy(u_ref.at[pl.ds(c * step, step)], u_out.at[pl.ds(c * step, step)], keep_sem.at[1]))
         results[-1].start()
-        if c % 2 == 1:
-            advance(done[0])
+        advance(done[0])
+    for h in range(parts):
+        side_take(h)
     advance(pieces + 3)
     pltpu.make_async_copy(u_ref, u_out, keep_sem.at[1]).wait()
     everything = pl.ds(0, rows)
@@ -572,7 +678,9 @@
 
     for h in range(parts):
         plane[h][1][3].wait_send()
-    up, down, sibs = onward(everything, xr_ref, 0)
+    _, _, sibs = onward(everything, xr_ref, 0)
+    fewer = pl.ds(0, rows - rows // nc)
+    up, down, _ = onward(fewer, xr_ref.at[fewer], 0)
 
     @pl.when(goes_up)
     def _():
@@ -584,6 +692,7 @@
 
     for sib in sibs:
         sib.wait()
+    side_drain()
 
 
 def padded(count, unit):
@@ -605,7 +714,7 @@
     tall, flat = plane_shape(nc)
     sub = rows // (parts * nc)
     pieces = nc * parts
-    sems = 2 * 2 * 3 + 4 * parts + pieces + ratio + 1
+    sems = 2 * 2 * 3 + 4 * parts + pieces + ratio + 1 + nc * parts + 2 * nc
     f32 = jnp.float32
     vmem = pl.BlockSpec(memory_space=pltpu.VMEM)
     return pl.pallas_call(
@@ -632,7 +741,8 @@
             pltpu.VMEM((follow, BLK), f32),
             pltpu.VMEM((follow, BLK), f32),
             pltpu.VMEM((land1, BLK), f32),
-            pltpu.VMEM(((flat - 1) * tall * sub, size), f32),
+            pltpu.VMEM((nc, parts * sub, size), f32),
+            pltpu.VMEM((max((flat - 1) * tall, parts) * sub, size), f32),
             pltpu.VMEM((parts, flat - 1, tall, sub, size // 2), f32),
             pltpu.VMEM((parts, tall - 1, flat, sub, size // 2), f32),
             pltpu.VMEM((parts, tall, sub, size // 2), f32),

time: 102 us -> 94.7 us (0.928)
  Pallas kernels: 88 us -> 80.5 us
    pallas_call x1, Pallas kernels: 88 us -> 80.5 us  [exchange(): pl.pallas_call(functools.partial(kernel, nr, nc, parts, batches, foot), o...]
where the time goes in v3:
time: 94.7 us; the launch traced here: 94.3 us
  Pallas kernels  80.5 us (85%)
  matrix products  9.57 us (10%)
  local copies, waits for them, and re-layouts  2.14 us (2%)
  other arithmetic  1.51 us (2%)
    pallas_call x1, Pallas kernels, exchange(): pl.pallas_call(functools.partial(kernel, nr, nc, parts, batches, foot), o...  80.5 us
    dot_general x1, matrix products, on_device(): jnp.dot(u, cross_cols.reshape(cols_dev, total).T, precision=MID, preferre...  9.57 us

profile of v3, /device:TPU:7, one launch (start us, length us, event | category | flops | bytes accessed | tf_op | source)
XLA Modules:
  0.0 94.3 jit_solution(11164596906555521622)
XLA Ops:
  0.6 0.7 reshape.19
  1.3 0.7 convert_element_type.3
  2.0 0.7 reshape.18
  2.7 0.7 concatenate.3.pack_ref
  3.5 0.0 copy-start.1
  3.5 0.0 copy-start
  3.5 80.5 %shard_map.77 = (f32[1024,512]{1,0:T(8,128)S(1)}, f32[2,1024,512]{2,1,0:T(8,128)S(1)}, f32[8,128]{1,0:T(8,128)S(1)}) custom-call(f32[1024,2048]{1,0:T(8,128)} %p_ref.1, f32[24,256]{1,0:T(8,128)S(1)} %concatenate.3.pack_ref), custom_call_target="tpu_custom_call" | custom-call | tf_op jit(solution)/shard_map/pallas_call | solution.py:720
  83.9 0.2 multiply_reduce_fusion
  84.2 0.0 copy-done.1
  84.2 0.6 add.3
  84.8 0.0 copy-done
  84.8 9.6 %convolution_subtract_fusion = f32[1024,2048]{1,0:T(8,128)} fusion(f32[1024,2048]{1,0:T(8,128)S(1)} %copy-done, f32[1024,512]{1,0:T(8,128)S(1)} %get-tuple-element.5, f32[2048,512]{1,0:T(8,128)S(1)} %bitcast.5), kind=kOutput, calls=%fused_computation | convolution fusion | flops 6444548096 | bytes 23068672 | tf_op jit(solution)/shard_map/dot_general | solution.py:779
  (2 shorter events, 0.0 us)
Async XLA Ops:
  3.5 80.7 %copy-start.1 = (f32[1024]{0:T(1024)S(1)}, f32[1024]{0:T(1024)}, u32[]{:S(2)}) copy-start(f32[1024]{0:T(1024)} %param.7) | copy-start | bytes 12292
  3.5 81.3 %copy-start = (f32[1024,2048]{1,0:T(8,128)S(1)}, f32[1024,2048]{1,0:T(8,128)}, u32[]{:S(2)}) copy-start(f32[1024,2048]{1,0:T(8,128)} %p_ref.1) | copy-start | bytes 25165828

commit v4 on v3

--- a/solution.py
+++ b/solution.py
@@ -71,16 +71,16 @@
         winv = work[:, BLK:]
         ready(b)
         if hi < size:
-            panel = jnp.dot(winv, mat[lo:hi, hi:size], precision=HI, preferred_element_type=jnp.float32)
+            panel = jnp.dot(winv, mat[lo:hi, hi:size], precision=MID, preferred_element_type=jnp.float32)
         if lo > 0:
-            left = jnp.dot(winv, mat[lo:hi, size : size + lo], precision=HI, preferred_element_type=jnp.float32)
+            left = jnp.dot(winv, mat[lo:hi, size : size + lo], precision=MID, preferred_element_type=jnp.float32)
             mat[lo:hi, size : size + lo] = left
         mat[lo:hi, size + lo : size + hi] = winv
         if hi < size:
             right = mat[lo:hi, size : size + hi]
             dims = (((0,), (0,)), ((), ()))
-            mat[hi:size, hi:size] = mat[hi:size, hi:size] - lax.dot_general(panel, panel, dims, precision=HI, preferred_element_type=jnp.float32)
-            mat[hi:size, size : size + hi] = mat[hi:size, size : size + hi] - lax.dot_general(panel, right, dims, precision=HI, preferred_element_type=jnp.float32)
+            mat[hi:size, hi:size] = mat[hi:size, hi:size] - lax.dot_general(panel, panel, dims, precision=MID, preferred_element_type=jnp.float32)
+            mat[hi:size, size : size + hi] = mat[hi:size, size : size + hi] - lax.dot_general(panel, right, dims, precision=MID, preferred_element_type=jnp.float32)
 
 
 def pair_blocks(size):
@@ -195,7 +195,7 @@
     hi, lo = col // flat, col % flat
     half = size // 2
     left, right = pl.ds(0, half), pl.ds(half, half)
-    chain_base = take(pieces)
+    chain_base = send_sem.shape[0]
     sib_base = take(ratio - 1)
     up_sem, down_sem = sib_base + ratio - 1, sib_base + ratio
     take(2)
@@ -340,7 +340,7 @@
         up.wait_recv()
         send_on(e, up, down, sibs)
 
-    side_recv = take(nc * parts)
+    side_recv = chain_base + pieces
     side_send = take(2 * nc)
     last_up = jnp.logical_and(col == top, high < top)
     last_down = jnp.logical_and(col == 0, high > 0)
@@ -590,6 +590,7 @@
         if parts > 2 and slot == 2:
             settle(2)
         if slot == 3:
+            next(rest)
             arrive(1)
             emit(group(1))
         if parts > 2:
@@ -613,7 +614,6 @@
 
     def ready(b):
         if b == 0:
-            next(rest)
             point(3)
             if parts > 2:
                 spread(2)
@@ -714,7 +714,8 @@
     tall, flat = plane_shape(nc)
     sub = rows // (parts * nc)
     pieces = nc * parts
-    sems = 2 * 2 * 3 + 4 * parts + pieces + ratio + 1 + nc * parts + 2 * nc
+    sends = 2 * 2 * 3 - 1 + 4 * parts + ratio + 1 + 2 * nc
+    receives = sends + pieces + nc * parts
     f32 = jnp.float32
     vmem = pl.BlockSpec(memory_space=pltpu.VMEM)
     return pl.pallas_call(
@@ -751,8 +752,8 @@
             pltpu.VMEM((parts, flat - 1, sub, size // 2), f32),
             pltpu.VMEM((size, 2 * size), f32),
             pltpu.VMEM((BLK, 2 * BLK), f32),
-            pltpu.SemaphoreType.DMA((sems,)),
-            pltpu.SemaphoreType.DMA((sems,)),
+            pltpu.SemaphoreType.DMA((sends,)),
+            pltpu.SemaphoreType.DMA((receives,)),
             pltpu.SemaphoreType.DMA((parts,)),
         ],
         compiler_params=pltpu.CompilerParams(collective_id=0, has_side_effects=True, vmem_limit_bytes=40 * 1024 * 1024),

time: 94.7 us -> 92 us (0.971)
  Pallas kernels: 80.5 us -> 77.8 us
    pallas_call x1, Pallas kernels: 80.5 us -> 77.8 us  [exchange(): pl.pallas_call(functools.partial(kernel, nr, nc, parts, batches, foot), o...]
where the time goes in v4:
time: 92 us; the launch traced here: 91.6 us
  Pallas kernels  77.8 us (85%)
  matrix products  9.57 us (10%)
  local copies, waits for them, and re-layouts  2.14 us (2%)
  other arithmetic  1.51 us (2%)
    pallas_call x1, Pallas kernels, exchange(): pl.pallas_call(functools.partial(kernel, nr, nc, parts, batches, foot), o...  77.8 us
    dot_general x1, matrix products, on_device(): jnp.dot(u, cross_cols.reshape(cols_dev, total).T, precision=MID, preferre...  9.57 us

profile of v4, /device:TPU:7, one launch (start us, length us, event | category | flops | bytes accessed | tf_op | source)
XLA Modules:
  0.0 91.6 jit_solution(7622038551488895587)
XLA Ops:
  0.6 0.7 reshape.19
  1.3 0.7 convert_element_type.3
  2.0 0.7 reshape.18
  2.7 0.7 concatenate.3.pack_ref
  3.5 0.0 copy-start.1
  3.5 0.0 copy-start
  3.5 77.8 %shard_map.77 = (f32[1024,512]{1,0:T(8,128)S(1)}, f32[2,1024,512]{2,1,0:T(8,128)S(1)}, f32[8,128]{1,0:T(8,128)S(1)}) custom-call(f32[1024,2048]{1,0:T(8,128)} %p_ref.1, f32[24,256]{1,0:T(8,128)S(1)} %concatenate.3.pack_ref), custom_call_target="tpu_custom_call" | custom-call | tf_op jit(solution)/shard_map/pallas_call | solution.py:721
  81.2 0.2 multiply_reduce_fusion
  81.5 0.0 copy-done.1
  81.5 0.6 add.3
  82.1 0.0 copy-done
  82.1 9.6 %convolution_subtract_fusion = f32[1024,2048]{1,0:T(8,128)} fusion(f32[1024,2048]{1,0:T(8,128)S(1)} %copy-done, f32[1024,512]{1,0:T(8,128)S(1)} %get-tuple-element.5, f32[2048,512]{1,0:T(8,128)S(1)} %bitcast.5), kind=kOutput, calls=%fused_computation | convolution fusion | flops 6444548096 | bytes 23068672 | tf_op jit(solution)/shard_map/dot_general | solution.py:780
  (2 shorter events, 0.0 us)
Async XLA Ops:
  3.5 78.0 %copy-start.1 = (f32[1024]{0:T(1024)S(1)}, f32[1024]{0:T(1024)}, u32[]{:S(2)}) copy-start(f32[1024]{0:T(1024)} %param.7) | copy-start | bytes 12292
  3.5 78.6 %copy-start = (f32[1024,2048]{1,0:T(8,128)S(1)}, f32[1024,2048]{1,0:T(8,128)}, u32[]{:S(2)}) copy-start(f32[1024,2048]{1,0:T(8,128)} %p_ref.1) | copy-start | bytes 25165828

commit v5 on v4

--- a/solution.py
+++ b/solution.py
@@ -50,7 +50,7 @@
         lane = lax.broadcasted_iota(jnp.int32, (PANEL, BLK), 1)
         lhs = jnp.where(lane >= start + PANEL, left, 0.0)
         work[pl.ds(start, PANEL), :] = both
-        work[first:, :] = work[first:, :] - lax.dot_general(lhs[:, first:], both, (((0,), (0,)), ((), ())), precision=HI, preferred_element_type=jnp.float32)
+        work[first:, :] = work[first:, :] - lax.dot_general(lhs[:, first:], both, (((0,), (0,)), ((), ())), precision=MID, preferred_element_type=jnp.float32)
         return carry
 
     steps = BLK // PANEL // 4
@@ -576,9 +576,8 @@
         8: [(side_deliver, 0, 2), (side_deliver, 1, 2), (side_forward, 0, 3), (side_forward, 1, 3), (side_deliver, 0, 3), (side_deliver, 1, 3)],
         9: [(side_forward, 2, 2), (side_deliver, 2, 1), (side_deliver, 3, 1)],
         11: [(side_forward, 3, 2)],
-        12: [(side_deliver, 2, 2), (side_deliver, 3, 2)],
-        14: [(side_forward, 2, 3), (side_deliver, 2, 3)],
-        15: [(side_forward, 3, 3), (side_deliver, 3, 3)],
+        12: [(side_deliver, 2, 2), (side_deliver, 3, 2), (side_forward, 2, 3), (side_deliver, 2, 3)],
+        14: [(side_forward, 3, 3), (side_deliver, 3, 3)],
     }
 
     def hook(slot):

time: 92 us -> 92.2 us (level)
  no operation moved by 1% of the time
where the time goes in v5:
time: 92.2 us; the launch traced here: 91.8 us
  Pallas kernels  78 us (85%)
  matrix products  9.57 us (10%)
  local copies, waits for them, and re-layouts  2.14 us (2%)
  other arithmetic  1.51 us (2%)
    pallas_call x1, Pallas kernels, exchange(): pl.pallas_call(functools.partial(kernel, nr, nc, parts, batches, foot), o...  78 us
    dot_general x1, matrix products, on_device(): jnp.dot(u, cross_cols.reshape(cols_dev, total).T, precision=MID, preferre...  9.57 us

profile of v5, /device:TPU:7, one launch (start us, length us, event | category | flops | bytes accessed | tf_op | source)
XLA Modules:
  0.0 91.8 jit_solution(12985646553289634501)
XLA Ops:
  0.6 0.7 reshape.19
  1.3 0.7 convert_element_type.3
  2.0 0.7 reshape.18
  2.7 0.7 concatenate.3.pack_ref
  3.5 0.0 copy-start.1
  3.5 0.0 copy-start
  3.5 78.0 %shard_map.77 = (f32[1024,512]{1,0:T(8,128)S(1)}, f32[2,1024,512]{2,1,0:T(8,128)S(1)}, f32[8,128]{1,0:T(8,128)S(1)}) custom-call(f32[1024,2048]{1,0:T(8,128)} %p_ref.1, f32[24,256]{1,0:T(8,128)S(1)} %concatenate.3.pack_ref), custom_call_target="tpu_custom_call" | custom-call | tf_op jit(solution)/shard_map/pallas_call | solution.py:720
  81.5 0.2 multiply_reduce_fusion
  81.7 0.0 copy-done.1
  81.7 0.6 add.3
  82.3 0.0 copy-done
  82.3 9.6 %convolution_subtract_fusion = f32[1024,2048]{1,0:T(8,128)} fusion(f32[1024,2048]{1,0:T(8,128)S(1)} %copy-done, f32[1024,512]{1,0:T(8,128)S(1)} %get-tuple-element.5, f32[2048,512]{1,0:T(8,128)S(1)} %bitcast.5), kind=kOutput, calls=%fused_computation | convolution fusion | flops 6444548096 | bytes 23068672 | tf_op jit(solution)/shard_map/dot_general | solution.py:779
  (2 shorter events, 0.0 us)
Async XLA Ops:
  3.5 78.2 %copy-start.1 = (f32[1024]{0:T(1024)S(1)}, f32[1024]{0:T(1024)}, u32[]{:S(2)}) copy-start(f32[1024]{0:T(1024)} %param.7) | copy-start | bytes 12292
  3.5 78.8 %copy-start = (f32[1024,2048]{1,0:T(8,128)S(1)}, f32[1024,2048]{1,0:T(8,128)}, u32[]{:S(2)}) copy-start(f32[1024,2048]{1,0:T(8,128)} %p_ref.1) | copy-start | bytes 25165828
